TPU v7x, 32 devices: a whole 2x2x4 slice. The times are simulated.
32 devices in a mesh: rep: 2 (over y), grp: 16 (over z, x, core).
Axes of the slice: x: 2, y: 2, z: 4, core: 2. Of those that a mesh axis runs over, the one named last changes fastest.
Arguments:
- block_input: bfloat16 [32768, 768], P(('rep', 'grp')), may hold values from -6 to 6
- prev_logits: float32 [32768, 8], P(('rep', 'grp')), may hold values from -6 to 6
- routes: int32 [32768, 2], P(('rep', 'grp')), may hold values from 0 to 7, all different within a row; in each aligned block of 512 rows (0 to 511, 512 to 1023, ...) at most 256 rows name the same one
- segments: int32 [64, 512], P(('rep', 'grp')), may hold values from 0 to 3, never falling along the last dimension, each value on 1 to 256 neighbouring positions
- grad_out: bfloat16 [32768, 768], P(('rep', 'grp')), may hold values from -6 to 6
- gain_attn: float32 [768], P('grp'), may hold values from 0.5 to 1.5
- w_query: float32 [768, 768], P('grp'), may hold values from -0.21875 to 0.21875
- w_key: float32 [768, 768], P('grp'), may hold values from -0.21875 to 0.21875
- w_value: float32 [768, 768], P('grp'), may hold values from -0.21875 to 0.21875
- w_output: float32 [768, 768], P('grp'), may hold values from -0.875 to 0.875
- gain_mix: float32 [768], P('grp'), may hold values from 0.5 to 1.5
- router: float32 [768, 8], P('grp'), may hold values from -0.21650635 to 0.21650635
- route_map: float32 [8, 8], replicated, may hold values from -1.2 to 1.2
- const_proj: float32 [768, 4], P('grp'), may hold values from -0.21875 to 0.21875
- const_vec: float32 [768, 2], P('grp'), may hold values from -6 to 6
- w_gate: float32 [768, 4, 2048], P('grp'), may hold values from -0.21875 to 0.21875
- w_up: float32 [768, 4, 2048], P('grp'), may hold values from -0.21875 to 0.21875
- w_down: float32 [2048, 4, 768], P('grp'), may hold values from -0.25 to 0.25
Outputs:
- block_output: float32 [32768, 768], P(('rep', 'grp'))
- grad_input: float32 [32768, 768], P(('rep', 'grp'))
- grad_gain_attn: float32 [768], P('grp')
- grad_w_query: float32 [768, 768], P('grp')
- grad_w_key: float32 [768, 768], P('grp')
- grad_w_value: float32 [768, 768], P('grp')
- grad_w_output: float32 [768, 768], P('grp')
- grad_gain_mix: float32 [768], P('grp')
- grad_router: float32 [768, 8], P('grp')
- grad_route_map: float32 [8, 8], replicated
- grad_const_proj: float32 [768, 4], P('grp')
- grad_const_vec: float32 [768, 2], P('grp')
- grad_w_gate: float32 [768, 4, 2048], P('grp')
- grad_w_up: float32 [768, 4, 2048], P('grp')
- grad_w_down: float32 [2048, 4, 768], P('grp')
Inputs may be any that keep to these rules, and one draw needn't show every extreme that they name: `routes`: each row names two different experts; within one sequence no expert is named by more than 256 tokens. `segments`: document numbers never fall along a sequence; a document has at most 256 tokens.
All inputs are finite; a program needn't handle non-finite values.
Results may differ from a plain program's by a relative error of at most 0.017.
Values may be sent and summed in bfloat16 or wider, within the bound.
A program may use at most 448 MiB of HBM per device.

v0:
```python
import functools

import jax
import jax.numpy as jnp
import numpy as np
from jax import lax
from jax.experimental import pallas as pl
from jax.experimental.pallas import tpu as pltpu
from jax.sharding import PartitionSpec as P

HEAD_DIM = 64
BLOCK = 256
EPS = 1e-05
NEG = -1000000000.0
F32 = jnp.float32
BF16 = jnp.bfloat16
LANES = 128


def nn(a, b):
    return lax.dot_general(a, b, (((1,), (0,)), ((), ())), preferred_element_type=F32)


def nt(a, b):
    return lax.dot_general(a, b, (((1,), (1,)), ((), ())), preferred_element_type=F32)


def tn(a, b):
    return lax.dot_general(a, b, (((0,), (0,)), ((), ())), preferred_element_type=F32)


def iota(shape, dim):
    return lax.broadcasted_iota(jnp.int32, shape, dim)


def split2(values):
    high = values.astype(BF16)
    low = (values - high.astype(F32)).astype(BF16)
    return high, low


def whole(shape, buffers=None):
    zeros = (0,) * len(shape)
    if buffers:
        return pl.BlockSpec(shape, lambda *_: zeros, pipeline_mode=pl.Buffered(buffers))
    return pl.BlockSpec(shape, lambda *_: zeros)


def per_seq(shape):
    tail = (0,) * len(shape)
    return pl.BlockSpec((1,) + shape, lambda b, *_: (b,) + tail)


def same_document(segments):
    hot = jnp.where(segments == iota((16, segments.shape[1]), 0), 1.0, 0.0).astype(BF16)
    return tn(hot, hot) > 0.5


def rms_scale(values):
    return lax.rsqrt(jnp.mean(values * values, axis=-1, keepdims=True) + EPS)


def slot_mask(position_row, capacity):
    places = iota((capacity, position_row.shape[1]), 0).astype(F32)
    return jnp.where(places == position_row, 1.0, 0.0).astype(BF16)


def grad_rows_kernel(own_ref, routes_ref, grad_ref, r0, r1, r2, r3, pos_ref):
    own = own_ref[0]
    kinds, length = pos_ref.shape[1:]
    capacity = r0.shape[1]
    ids = iota((kinds, length), 0)
    first = routes_ref[0:1, :] == ids
    second = routes_ref[1:2, :] == ids
    hits = jnp.where(first | second, 1.0, 0.0)
    before = jnp.where(iota((length, length), 0) < iota((length, length), 1), 1.0, 0.0)
    slots = nn(hits.astype(BF16), before.astype(BF16))
    pos_ref[0] = jnp.where(hits > 0.0, slots, -1.0)
    for number, rows in enumerate((r0, r1, r2, r3)):
        line = pos_ref[0, pl.ds(own ^ number, 1), :]
        rows[0] = nn(slot_mask(line, capacity), grad_ref[0]).astype(BF16)


def swap_halves(values, low_half):
    return jnp.where(low_half, pltpu.roll(values, 96, 1), pltpu.roll(values, 32, 1))


def sequence_forward(
    x_ref,
    segments,
    routes,
    prev_ref,
    map_ref,
    small_ref,
    wq_ref,
    wk_ref,
    wv_ref,
    wo_ref,
    cos_ref,
    sin_ref,
    pos_ref,
    q_ref,
    k_ref,
    v_ref,
    o_ref,
    h_ref,
    lse_ref,
    aux_ref,
    rows_at,
    bias_ref,
    proj_ref,
    expert_of,
    between=None,
):
    length, width = x_ref.shape[1:]
    kinds = pos_ref.shape[1]
    capacity = length // 2
    tokens = x_ref[0].astype(F32)
    gain_one = small_ref[kinds + 6 : kinds + 7, :]
    gain_two = small_ref[kinds + 7 : kinds + 8, :]
    a1 = (tokens * rms_scale(tokens) * gain_one).astype(BF16)
    lane = iota((1, LANES), 1)
    low_half = (lane % HEAD_DIM) < (HEAD_DIM // 2)
    first_head = lane < HEAD_DIM
    mask_a = jnp.where(first_head, 1.0, 0.0).astype(BF16)
    mask_b = jnp.where(first_head, 0.0, 1.0).astype(BF16)
    pairs = width // LANES

    for weights, target, scale in ((wq_ref, q_ref, 0.125), (wk_ref, k_ref, 1.0)):
        proj_ref[...] = nn(a1, weights[...])

        def turn(h, carry):
            cols = pl.ds(pl.multiple_of(h * LANES, LANES), LANES)
            part = proj_ref[:, cols]
            turned = part * cos_ref[...] + swap_halves(part, low_half) * sin_ref[...]
            target[0, :, cols] = turned.astype(BF16) * jnp.asarray(scale, BF16)
            return carry

        lax.fori_loop(0, pairs, turn, 0)
    v_ref[0] = nn(a1, wv_ref[...]).astype(BF16)

    allowed = same_document(segments) & (
        iota((length, length), 1) // BLOCK <= iota((length, length), 0) // BLOCK
    )
    bias_ref[...] = jnp.where(allowed, 0.0, NEG)
    lse_ref[...] = jnp.zeros_like(lse_ref)
    if between is not None:
        between()

    def pair(h, carry):
        cols = pl.ds(pl.multiple_of(h * LANES, LANES), LANES)
        for begin in range(0, length, BLOCK):
            end = begin + BLOCK
            queries = q_ref[0, begin:end, cols]
            keys = k_ref[0, 0:end, cols]
            values = v_ref[0, 0:end, cols]
            bias = bias_ref[begin:end, 0:end]
            sums = lse_ref[0, begin:end, :]
            outs = []
            for half, mask in enumerate((mask_a, mask_b)):
                scores = nt(queries * mask, keys) + bias
                top = jnp.max(scores, axis=-1, keepdims=True)
                grown = jnp.exp(scores - top)
                total = jnp.sum(grown, axis=-1, keepdims=True)
                chances = (grown * (1.0 / total)).astype(BF16)
                outs.append(nn(chances, values))
                sums = jnp.where(lane == 2 * h + half, top + jnp.log(total), sums)
            lse_ref[0, begin:end, :] = sums
            o_ref[0, begin:end, cols] = jnp.where(first_head, outs[0], outs[1]).astype(BF16)
        return carry

    lax.fori_loop(0, pairs, pair, 0)

    hidden = tokens + nn(o_ref[0], wo_ref[...])
    h_ref[0] = hidden
    a2 = (hidden * rms_scale(hidden) * gain_two).astype(BF16)
    logits = nt(small_ref[...].astype(BF16), a2)[0:kinds, :]
    for j in range(kinds):
        logits = logits + map_ref[:, j : j + 1] * prev_ref[j : j + 1, :]
    ids = iota((kinds, length), 0)
    first = jnp.where(routes[0:1, :] == ids, 1.0, 0.0)
    second = jnp.where(routes[1:2, :] == ids, 1.0, 0.0)
    one = jnp.sum(logits * first, axis=0, keepdims=True)
    two = jnp.sum(logits * second, axis=0, keepdims=True)
    top = jnp.maximum(one, two)
    grown_one, grown_two = jnp.exp(one - top), jnp.exp(two - top)
    gate_one = grown_one / (grown_one + grown_two)
    gate_two = grown_two / (grown_one + grown_two)
    aux_ref[0, 0:kinds, :] = gate_one * first + gate_two * second
    aux_ref[0, kinds : kinds + 1, :] = gate_one
    aux_ref[0, kinds + 1 : kinds + 2, :] = gate_two
    aux_ref[0, kinds + 2 : kinds + 4, :] = routes.astype(F32)
    aux_ref[0, kinds + 4 :, :] = jnp.zeros((aux_ref.shape[1] - kinds - 4, length), F32)

    place = iota((16, length), 0)

    def send_rows(number, carry):
        rows = rows_at(number)
        mask = slot_mask(pos_ref[0, pl.ds(expert_of(number), 1), :], capacity)
        rows[0, 0:capacity, :] = nn(mask, a2).astype(BF16)
        line = aux_ref[0, pl.ds(expert_of(number), 1), :]
        high = line.astype(BF16).astype(F32)
        mid = (line - high).astype(BF16).astype(F32)
        low = line - high - mid
        parts = jnp.where(place == 0, high, jnp.where(place == 1, mid, jnp.where(place == 2, low, 0.0)))
        spread = nt(parts.astype(BF16), mask)
        filled = jnp.max(pos_ref[0, pl.ds(expert_of(number), 1), :], axis=1, keepdims=True) + 1.0
        spread = jnp.where(iota((16, 1), 0) == 3, filled, spread)
        rows[0, capacity:, 0:capacity] = spread.astype(BF16)
        rows[0, capacity:, capacity:] = jnp.zeros((16, width - capacity), BF16)
        return carry

    lax.fori_loop(0, 4, send_rows, 0)


def forward_kernel(
    own_ref,
    x_ref,
    seg_ref,
    routes_ref,
    prev_ref,
    map_ref,
    small_ref,
    wq_ref,
    wk_ref,
    wv_ref,
    wo_ref,
    cos_ref,
    sin_ref,
    pos_ref,
    q_ref,
    k_ref,
    v_ref,
    o_ref,
    h_ref,
    lse_ref,
    aux_ref,
    rows_ref,
    bias_ref,
    proj_ref,
):
    own = own_ref[0]
    sequence_forward(
        x_ref,
        seg_ref[0],
        routes_ref[...],
        prev_ref,
        map_ref,
        small_ref,
        wq_ref,
        wk_ref,
        wv_ref,
        wo_ref,
        cos_ref,
        sin_ref,
        pos_ref,
        q_ref,
        k_ref,
        v_ref,
        o_ref,
        h_ref,
        lse_ref,
        aux_ref,
        lambda number: rows_ref.at[number],
        bias_ref,
        proj_ref,
        lambda number: own ^ number,
    )


MESH = pl.DeviceIdType.MESH


class Place:
    def __init__(self, group):
        self.group = group
        self.planes = group // 4
        self.g = lax.axis_index("grp")
        self.y = lax.axis_index("rep")
        self.core = self.g % 2
        self.x = (self.g // 2) % 2
        self.z = self.g // 4
        self.core_peer = (self.y, self.g + 1 - 2 * self.core)
        self.x_peer = (self.y, self.g + 2 - 4 * self.x)
        self.y_peer = (1 - self.y, self.g)
        self.xy_peer = (1 - self.y, self.g + 2 - 4 * self.x)
        self.plane_peers = (None, self.x_peer, self.y_peer, self.xy_peer)

    def z_peer(self, k):
        return (self.y, (self.g + 4 * k) % self.group)

    def block(self, z, x, core):
        return (z * 2 + x) * 2 + core

    def expert(self, number):
        return 2 * ((self.y + number // 2) % 2) + (self.x + number % 2) % 2

    def barrier(self, peers):
        semaphore = pltpu.get_barrier_semaphore()
        for peer in peers:
            pl.semaphore_signal(semaphore, inc=1, device_id=peer, device_id_type=MESH)
        pl.semaphore_wait(semaphore, len(peers))


def remote(src, dst, send, recv, peer):
    return pltpu.make_async_remote_copy(
        src_ref=src, dst_ref=dst, send_sem=send, recv_sem=recv, device_id=peer, device_id_type=MESH
    )


def fused_forward_kernel(
    group,
    x_ref,
    seg_ref,
    routes_ref,
    prev_ref,
    map_ref,
    grad_ref,
    coarse_ref,
    fine_ref,
    shard_refs,
    small_refs,
    gate4_ref,
    up4_ref,
    down4_ref,
    q_ref,
    k_ref,
    v_ref,
    o_ref,
    h_ref,
    lse_ref,
    aux_ref,
    pos_ref,
    small_ref,
    cos_ref,
    sin_ref,
    attn_out_ref,
    attn_o_out_ref,
    rows_in_ref,
    grads_in_ref,
    gate_full_ref,
    up_full_ref,
    down_full_ref,
    attn_ref,
    attn_o_ref,
    bias_ref,
    proj_ref,
    rows_ref,
    grows_ref,
    tile_ref,
    map_t_ref,
    attn_send,
    attn_recv,
    ffn_local,
    ffn_send,
    ffn_recv,
    out_sem,
    row_local,
    row_send,
    row_recv,
):
    step = pl.program_id(0)
    last = pl.num_programs(0) - 1
    here = Place(group)
    planes = here.planes
    batches, kinds, length = pos_ref.shape
    width = x_ref.shape[2]
    capacity = length // 2
    shards = (attn_ref, attn_o_ref)
    experts = ((gate4_ref, gate_full_ref), (up4_ref, up_full_ref), (down4_ref, down_full_ref))
    depth = shard_refs[0].shape[0]
    mine = here.block(here.z, here.x, here.core)

    def rows_of(block):
        return pl.ds(pl.multiple_of(block * depth, 16), depth)

    def attn_part(t, block, part):
        full = shards[t]
        half = full.shape[1] // 2
        if part is None:
            return full.at[rows_of(block), :]
        return full.at[rows_of(block), pl.ds(pl.multiple_of(part * half, LANES), half)]

    def attn_copy(t, slot, z, x, part, peer):
        ref = attn_part(t, here.block(z, x, here.core), part)
        return remote(ref, ref, attn_send.at[t, slot], attn_recv.at[t, slot], peer)

    def to_z(t, k):
        return attn_copy(t, k, here.z, here.x, None, here.z_peer(1 if k == 0 else planes - 1))

    def from_z(t, k):
        return attn_copy(t, k, z_at(planes - 1 if k == 0 else 1), here.x, None, here.x_peer)

    def pass_z(t, k):
        z = z_at(planes - 1 if k == 0 else 1)
        return attn_copy(t, 2 + k, z, here.x, k, here.z_peer(1 if k == 0 else planes - 1))

    def passed_z(t, k):
        return attn_copy(t, 2 + k, z_at(2), here.x, k, here.x_peer)

    def to_x(t, step_z):
        return attn_copy(t, 4 + step_z, z_at(step_z), here.x, here.y, here.x_peer)

    def from_x(t, step_z):
        return attn_copy(t, 4 + step_z, z_at(step_z), 1 - here.x, here.y, here.x_peer)

    def to_y(t, step_z):
        return attn_copy(t, 4 + planes + step_z, z_at(step_z), 1 - here.x, here.y, here.y_peer)

    def from_y(t, step_z):
        return attn_copy(t, 4 + planes + step_z, z_at(step_z), 1 - here.x, 1 - here.y, here.y_peer)

    def to_core(t, step_z, x):
        return attn_copy(t, 4 + 2 * planes + 2 * step_z + x, z_at(step_z), here.x if x == 0 else 1 - here.x, None, here.core_peer)

    def from_core(t, step_z, x):
        ref = attn_part(t, here.block(z_at(step_z), here.x if x == 0 else 1 - here.x, 1 - here.core), None)
        slot = 4 + 2 * planes + 2 * step_z + x
        return remote(ref, ref, attn_send.at[t, slot], attn_recv.at[t, slot], here.core_peer)

    def z_at(k):
        return (here.z + k) % planes

    def ffn_to_x(j):
        source, full = experts[j]
        return remote(
            source.at[here.expert(1)],
            full.at[here.z, here.x, here.core],
            ffn_send.at[j, 0],
            ffn_recv.at[j, 0],
            here.x_peer,
        )

    def ffn_from_x(j):
        source, full = experts[j]
        return remote(
            source.at[here.expert(1)],
            full.at[here.z, 1 - here.x, here.core],
            ffn_send.at[j, 0],
            ffn_recv.at[j, 0],
            here.x_peer,
        )

    def ffn_mine(j):
        source, full = experts[j]
        return pltpu.make_async_copy(source.at[here.expert(0)], full.at[here.z, here.x, here.core], ffn_local.at[j])

    def ffn_copy(j, slot, z, x, core, peer):
        full = experts[j][1]
        part = full.at[z, :, core] if x is None else full.at[z, x, core]
        return remote(part, part, ffn_send.at[j, slot], ffn_recv.at[j, slot], peer)

    def ffn_to_z(j, k):
        return ffn_copy(j, 1 + k, here.z, None, here.core, here.z_peer(1 if k == 0 else planes - 1))

    def ffn_from_z(j, k):
        return ffn_copy(j, 1 + k, z_at(planes - 1 if k == 0 else 1), None, here.core, here.x_peer)

    def ffn_pass_z(j, k):
        z = z_at(planes - 1 if k == 0 else 1)
        return ffn_copy(j, 3 + k, z, k, here.core, here.z_peer(1 if k == 0 else planes - 1))

    def ffn_passed_z(j, k):
        return ffn_copy(j, 3 + k, z_at(2), k, here.core, here.x_peer)

    def ffn_to_core(j, step_z):
        return ffn_copy(j, 5 + step_z, z_at(step_z), None, here.core, here.core_peer)

    def ffn_from_core(j, step_z):
        return ffn_copy(j, 5 + step_z, z_at(step_z), None, 1 - here.core, here.core_peer)

    def row_copy(kind, member, number):
        source, target = ((grows_ref, grads_in_ref), (rows_ref, rows_in_ref))[kind]
        src, dst = source.at[member, number], target.at[number, member]
        if number == 0:
            return pltpu.make_async_copy(src, dst, row_local.at[kind, member])
        return remote(
            src,
            dst,
            row_send.at[kind, member, number],
            row_recv.at[kind, member, number],
            here.plane_peers[number],
        )

    def outs(t):
        full, target = ((attn_ref, attn_out_ref), (attn_o_ref, attn_o_out_ref))[t]
        return pltpu.make_async_copy(full, target, out_sem.at[t])

    @pl.when(step == 0)
    def _():
        for j in range(3):
            ffn_mine(j).start()
        for part in range(3):
            attn_ref[rows_of(mine), part * width : (part + 1) * width] = shard_refs[part][...].astype(BF16)
        attn_o_ref[rows_of(mine), :] = shard_refs[3][...].astype(BF16)
        tile_ref[...] = jnp.zeros_like(tile_ref)
        at = 0
        for part in small_refs:
            tile_ref[at : at + part.shape[0], 0:depth] = part[...]
            at += part.shape[0]
        tile_ref[at : at + kinds, 0:kinds] = map_ref[...]
        turned = jnp.transpose(tile_ref[...])
        map_t_ref[...] = pltpu.roll(turned[0:kinds, :], LANES - kinds - 8, 1)
        attn_ref[rows_of(mine), 3 * width : 3 * width + LANES] = turned[0:depth, :].astype(BF16)
        attn_ref[rows_of(mine), 3 * width + LANES :] = jnp.zeros((depth, LANES), BF16)
        here.barrier(
            [here.core_peer, here.x_peer, here.y_peer, here.xy_peer, here.z_peer(1), here.z_peer(planes - 1)]
        )
        for t in range(2):
            to_z(t, 0).start()
            to_z(t, 1).start()
            to_x(t, 0).start()
            to_core(t, 0, 0).start()
        for j in range(3):
            ffn_to_x(j).start()

        ids = iota((kinds, length), 0)
        before = jnp.where(iota((length, length), 0) < iota((length, length), 1), 1.0, 0.0).astype(BF16)
        for member in range(batches):
            first = routes_ref[0:1, member * length : (member + 1) * length] == ids
            second = routes_ref[1:2, member * length : (member + 1) * length] == ids
            hits = jnp.where(first | second, 1.0, 0.0)
            pos_ref[member] = jnp.where(hits > 0.0, nn(hits.astype(BF16), before), -1.0)

        def grad_rows(index, carry):
            member, number = index // 4, index % 4
            line = pos_ref[member, pl.ds(here.expert(number), 1), :]
            grows_ref[member, number] = nn(slot_mask(line, capacity), grad_ref[member]).astype(BF16)
            return carry

        lax.fori_loop(0, 4 * batches, grad_rows, 0)
        for member in range(batches):
            row_copy(0, member, 0).start()
            row_copy(0, member, 2).start()

        for high in range(coarse_ref.shape[1]):
            rows = slice(high * fine_ref.shape[1], (high + 1) * fine_ref.shape[1])
            cos_high, sin_high = coarse_ref[0, high : high + 1, :], coarse_ref[1, high : high + 1, :]
            cos_ref[rows, :] = cos_high * fine_ref[0] - sin_high * fine_ref[1]
            sin_ref[rows, :] = (sin_high * fine_ref[0] + cos_high * fine_ref[1]) * fine_ref[2]

        for t in range(2):
            for k, step_z in enumerate((planes - 1, 1)):
                from_z(t, k).wait_recv()
                pass_z(t, k).start()
                to_x(t, step_z).start()
                to_core(t, step_z, 0).start()
        for t in range(2):
            from_x(t, 0).wait_recv()
            to_y(t, 0).start()
        for j in range(3):
            ffn_mine(j).wait()
            ffn_from_x(j).wait_recv()
            ffn_to_z(j, 0).start()
            ffn_to_z(j, 1).start()
            ffn_to_core(j, 0).start()
        for t in range(2):
            passed_z(t, 0).wait_recv()
            passed_z(t, 1).wait_recv()
            to_x(t, 2).start()
            to_core(t, 2, 0).start()
        for member in range(batches):
            row_copy(0, member, 1).start()
            row_copy(0, member, 3).start()
        for t in range(2):
            for step_z in (planes - 1, 1, 2):
                from_x(t, step_z).wait_recv()
                to_y(t, step_z).start()
        for t in range(2):
            for step_z in (0, planes - 1, 1, 2):
                from_y(t, step_z).wait_recv()
                to_core(t, step_z, 1).start()
        for t in range(2):
            for step_z in range(planes):
                for x in range(2):
                    from_core(t, step_z, x).wait_recv()
        for t in range(2):
            outs(t).start()
        small_ref[...] = jnp.transpose(attn_ref[:, 3 * width : 3 * width + LANES].astype(F32))[0 : kinds + 8, :]

    def between():
        @pl.when(step == last)
        def _():
            for j in range(3):
                for k, step_z in enumerate((planes - 1, 1)):
                    ffn_from_z(j, k).wait_recv()
                    ffn_pass_z(j, k).start()
                    ffn_to_core(j, step_z).start()

    sequence_forward(
        x_ref,
        seg_ref[pl.ds(step, 1), :],
        routes_ref[:, pl.ds(pl.multiple_of(step * length, LANES), length)],
        prev_ref,
        map_t_ref,
        small_ref,
        attn_ref.at[:, 0:width],
        attn_ref.at[:, width : 2 * width],
        attn_ref.at[:, 2 * width : 3 * width],
        attn_o_ref,
        cos_ref,
        sin_ref,
        pos_ref.at[pl.ds(step, 1)],
        q_ref,
        k_ref,
        v_ref,
        o_ref,
        h_ref,
        lse_ref,
        aux_ref,
        lambda number: rows_ref.at[pl.ds(step, 1), number],
        bias_ref,
        proj_ref,
        here.expert,
        between,
    )
    for member in range(batches):

        @pl.when(step == member)
        def _():
            for number in range(4):
                row_copy(1, member, number).start()

    @pl.when(step == last)
    def _():
        for j in range(3):
            for k in range(2):
                ffn_passed_z(j, k).wait_recv()
            ffn_to_core(j, 2).start()
        for t in range(2):
            outs(t).wait()
            for k in range(2):
                to_z(t, k).wait_send()
                pass_z(t, k).wait_send()
            for step_z in range(planes):
                to_x(t, step_z).wait_send()
                to_y(t, step_z).wait_send()
                for x in range(2):
                    to_core(t, step_z, x).wait_send()
        for j in range(3):
            ffn_to_x(j).wait_send()
            for k in range(2):
                ffn_to_z(j, k).wait_send()
                ffn_pass_z(j, k).wait_send()
            for step_z in range(planes):
                ffn_to_core(j, step_z).wait_send()
                ffn_from_core(j, step_z).wait_recv()
        for kind in range(2):
            for member in range(batches):
                for number in range(4):
                    copy = row_copy(kind, member, number)
                    copy.wait()


def expert_kernel(
    a_ref,
    g_ref,
    gate_ref,
    up_ref,
    down_ref,
    v_ref,
    d_ref,
    grad_gate_ref,
    grad_up_ref,
    grad_down_ref,
    rows_ref,
    grads_ref,
    gates_ref,
    rows_t_ref,
    grads_t_ref,
    places_ref,
    acc_value_ref,
    acc_input_ref,
    acc_gate_ref,
    acc_up_ref,
    acc_down_ref,
    share_ref,
    sems,
):
    step = pl.program_id(0)
    last = pl.num_programs(0) - 1
    batches, capacity, width = g_ref.shape[1:]
    blocks = 4 * batches

    @pl.when(step == 0)
    def _():
        copies = []
        for number in range(4):
            rows, grads = a_ref.at[number], g_ref.at[number]
            for member in range(batches):
                block = number * batches + member
                span = pl.ds(block * capacity, capacity)
                copies.append(
                    pltpu.make_async_copy(
                        rows.at[member, pl.ds(capacity, 16), pl.ds(0, capacity)],
                        gates_ref.at[block],
                        sems.at[3 * block],
                    )
                )
                copies.append(
                    pltpu.make_async_copy(
                        rows.at[member, pl.ds(0, capacity), :], rows_ref.at[span, :], sems.at[3 * block + 1]
                    )
                )
                copies.append(
                    pltpu.make_async_copy(grads.at[member], grads_ref.at[span, :], sems.at[3 * block + 2])
                )
        for copy in copies:
            copy.start()
        for copy in copies:
            copy.wait()
        same = iota((capacity, capacity), 0) == iota((capacity, capacity), 1)
        spare = jnp.zeros((capacity, width), BF16)
        rows_ref[blocks * capacity :, :] = spare
        grads_ref[blocks * capacity :, :] = spare
        share_ref[...] = jnp.zeros_like(share_ref)

        def pack(block, place):
            span = pl.ds(pl.multiple_of(block * capacity, capacity), capacity)
            target = pl.ds(pl.multiple_of(place, 16), capacity)
            parts = gates_ref[block].astype(F32)
            count = jnp.max(parts[3:4, :]).astype(jnp.int32)
            line = jnp.sum(parts[0:3, :], axis=0, keepdims=True)
            column = jnp.sum(jnp.where(same, line, 0.0), axis=1, keepdims=True)
            rows = rows_ref[span, :]
            grads = (grads_ref[span, :].astype(F32) * column).astype(BF16)
            rows_ref[target, :] = rows
            grads_ref[target, :] = grads
            places_ref[block] = place
            return place + (count + 15) // 16 * 16

        total = lax.fori_loop(0, blocks, pack, 0)
        target = pl.ds(pl.multiple_of(total, 16), capacity)
        rows_ref[target, :] = spare
        grads_ref[target, :] = spare
        places_ref[blocks] = (total + capacity - 1) // capacity

        def turn(block, carry):
            span = pl.ds(pl.multiple_of(block * capacity, capacity), capacity)
            grads_t_ref[:, span] = jnp.transpose(grads_ref[span, :])
            rows_t_ref[:, span] = jnp.transpose(rows_ref[span, :])
            return carry

        lax.fori_loop(0, places_ref[blocks], turn, 0)

    acc_gate_ref[...] = jnp.zeros_like(acc_gate_ref)
    acc_up_ref[...] = jnp.zeros_like(acc_up_ref)
    acc_down_ref[...] = jnp.zeros_like(acc_down_ref)

    def work(block, carry):
        span = pl.ds(pl.multiple_of(block * capacity, capacity), capacity)
        rows = rows_ref[span, :]
        grads = grads_ref[span, :]
        gate = nn(rows, gate_ref[...])
        up = nn(rows, up_ref[...])
        back = nt(grads, down_ref[...])
        sig = 1.0 / (1.0 + jnp.exp(-gate))
        silu = gate * sig
        act = (silu * up).astype(BF16)
        grad_gate = (back * up * (sig * (1.0 + gate * (1.0 - sig)))).astype(BF16)
        grad_up = (back * silu).astype(BF16)
        value = nn(act, down_ref[...])
        grad_rows = nt(grad_gate, gate_ref[...]) + nt(grad_up, up_ref[...])
        rows_t = rows_t_ref[:, span]
        acc_gate_ref[...] += nn(rows_t, grad_gate)
        acc_up_ref[...] += nn(rows_t, grad_up)
        acc_down_ref[...] += nn(grads_t_ref[:, span], act)
        share = jnp.broadcast_to(
            jnp.sum(act.astype(F32) * back, axis=1, keepdims=True), (capacity, LANES)
        )

        @pl.when(step == 0)
        def _():
            share_ref[span, :] = share
            acc_value_ref[span, :] = value
            acc_input_ref[span, :] = grad_rows

        @pl.when(step > 0)
        def _():
            share_ref[span, :] += share

        @pl.when((step > 0) & (step < last))
        def _():
            acc_value_ref[span, :] += value
            acc_input_ref[span, :] += grad_rows

        @pl.when(step == last)
        def _():
            rows_ref[span, :] = (acc_value_ref[span, :] + value).astype(BF16)
            grads_ref[span, :] = (acc_input_ref[span, :] + grad_rows).astype(BF16)

        return carry

    lax.fori_loop(0, places_ref[blocks], work, 0)
    grad_gate_ref[...] = acc_gate_ref[...].astype(BF16)
    grad_up_ref[...] = acc_up_ref[...].astype(BF16)
    grad_down_ref[...] = jnp.transpose(acc_down_ref[...].astype(BF16))

    @pl.when(step == last)
    def _():
        same = iota((capacity, capacity), 0) == iota((capacity, capacity), 1)
        place = iota((16, capacity), 0)

        def shares(block, carry):
            column = share_ref[pl.ds(pl.multiple_of(places_ref[block], 16), capacity), 0:1]
            line = jnp.sum(jnp.where(same, column, 0.0), axis=0, keepdims=True)
            high = line.astype(BF16).astype(F32)
            mid = (line - high).astype(BF16).astype(F32)
            low = line - high - mid
            parts = jnp.where(place == 0, high, jnp.where(place == 1, mid, jnp.where(place == 2, low, 0.0)))
            gates_ref[block] = parts.astype(BF16)
            return carry

        lax.fori_loop(0, blocks, shares, 0)
        copies = []
        for number in range(4):
            values, grads = v_ref.at[number], d_ref.at[number]
            for member in range(batches):
                block = number * batches + member
                span = pl.ds(pl.multiple_of(places_ref[block], 16), capacity)
                copies.append(pltpu.make_async_copy(rows_ref.at[span, :], values.at[member], sems.at[3 * block]))
                copies.append(
                    pltpu.make_async_copy(
                        grads_ref.at[span, :], grads.at[member, pl.ds(0, capacity), :], sems.at[3 * block + 1]
                    )
                )
                copies.append(
                    pltpu.make_async_copy(
                        gates_ref.at[block],
                        grads.at[member, pl.ds(capacity, 16), pl.ds(0, capacity)],
                        sems.at[3 * block + 2],
                    )
                )
        for copy in copies:
            copy.start()
        for copy in copies:
            copy.wait()


def constant_mix(zs, index):
    za, zb = zs[:, index : index + 1], zs[:, index + 1 : index + 2]
    top = jnp.maximum(za, zb)
    ea, eb = jnp.exp(za - top), jnp.exp(zb - top)
    return ea / (ea + eb), eb / (ea + eb)


def token_columns(pos_ref, aux_ref, cols_ref):
    kinds, length = pos_ref.shape[1:]
    cols_ref[0:kinds, :] = pos_ref[0]
    cols_ref[kinds : kinds + 16, :] = aux_ref[0]
    cols_ref[kinds + 16 :, :] = jnp.zeros((LANES - kinds - 16, length), F32)
    return jnp.transpose(cols_ref[...])


def column(source, index):
    return jnp.sum(jnp.where(iota((1, LANES), 1) == index, source, 0.0), axis=1, keepdims=True)


def result_kernel(own_ref, v_ref, pos_ref, aux_ref, h_ref, small_ref, out_ref, cols_ref):
    block_output(own_ref, v_ref, pos_ref, aux_ref, h_ref, small_ref, out_ref, cols_ref)


def finish_kernel(
    own_ref,
    v_ref,
    pos_ref,
    aux_ref,
    h_ref,
    small_ref,
    sums_ref,
    out_ref,
    gq_ref,
    gk_ref,
    gv_ref,
    go_ref,
    router_ref,
    proj_ref,
    vec_ref,
    gain_one_ref,
    gain_two_ref,
    map_ref,
    cols_ref,
    tile_ref,
):
    @pl.when(pl.program_id(0) == 0)
    def _():
        depth, width = gq_ref.shape
        kinds = pos_ref.shape[1]
        for part, ref in enumerate((gq_ref, gk_ref, gv_ref, go_ref)):
            ref[...] = sums_ref[:, part * width : (part + 1) * width]
        small = sums_ref[:, 4 * width : 4 * width + LANES]
        tile_ref[...] = jnp.zeros_like(tile_ref)
        tile_ref[0:depth, :] = small
        turned = jnp.transpose(tile_ref[...])
        at = 0
        for ref in (router_ref, proj_ref, vec_ref, gain_one_ref, gain_two_ref):
            ref[...] = turned[at : at + ref.shape[0], 0:depth]
            at += ref.shape[0]
        map_ref[...] = pltpu.roll(small[0:kinds, :], LANES - kinds - 8, 1)[:, 0:kinds]

    block_output(own_ref, v_ref, pos_ref, aux_ref, h_ref, small_ref, out_ref, cols_ref)


def block_output(own_ref, v_ref, pos_ref, aux_ref, h_ref, small_ref, out_ref, cols_ref):
    own = own_ref[0]
    length, width = h_ref.shape[1:]
    kinds = pos_ref.shape[1]
    ffn = kinds - 4
    capacity = v_ref.shape[2]
    hidden = h_ref[0]
    n2 = hidden * rms_scale(hidden) * small_ref[kinds + 7 : kinds + 8, :]
    n2_high, n2_low = split2(n2)
    small = small_ref[...].astype(BF16)
    cols = token_columns(pos_ref, aux_ref, cols_ref)
    out_ref[0] = hidden
    slot_lane = iota((1, capacity), 1).astype(F32)

    def take(number, carry):
        expert = own ^ number
        mask = jnp.where(column(cols, expert) == slot_lane, 1.0, 0.0).astype(BF16)
        out_ref[0] += column(cols, kinds + expert) * nn(mask, v_ref[number, 0])
        return carry

    lax.fori_loop(0, 4, take, 0)
    result = out_ref[0]
    mixes = nt(n2_high, small) + nt(n2_low, small)
    share = column(cols, kinds + ffn + 1)
    for constant in range(2):
        weight = column(cols, kinds + ffn + 2 + constant)
        alpha_a, alpha_b = constant_mix(mixes, kinds + 2 * constant)
        result = result + (weight * alpha_b) * small_ref[kinds + 4 + constant : kinds + 5 + constant, :]
        share = share + weight * alpha_a
    out_ref[0] = result + share * n2


def sequence_combine(
    step,
    d_ref,
    pos_ref,
    aux_ref,
    prev_ref,
    h_ref,
    g_ref,
    o_ref,
    small_ref,
    wo_ref,
    dh_ref,
    dob_ref,
    sgrad_ref,
    grad_map_ref,
    acc_ref,
    cols_ref,
    expert_of,
):
    length, width = h_ref.shape[1:]
    kinds = pos_ref.shape[1]
    ffn = kinds - 4
    capacity = d_ref.shape[2] - 16
    hidden = h_ref[0]
    inverse = rms_scale(hidden)
    gain = small_ref[kinds + 7 : kinds + 8, :]
    n2 = hidden * inverse * gain
    n2_high, n2_low = split2(n2)
    grad_low = g_ref[0]
    grad = grad_low.astype(F32)
    small = small_ref[...].astype(BF16)
    cols = token_columns(pos_ref, aux_ref, cols_ref)
    lane = iota((1, LANES), 1)
    gate_one = column(cols, 2 * kinds)
    gate_two = column(cols, 2 * kinds + 1)
    ids = lane.astype(F32)
    hot_one = jnp.where(column(cols, 2 * kinds + 2) == ids, 1.0, 0.0)
    hot_two = jnp.where(column(cols, 2 * kinds + 3) == ids, 1.0, 0.0)

    dh_ref[0] = jnp.zeros((length, width), F32)
    slot_lane = iota((1, capacity), 1).astype(F32)

    def take(number, shares):
        expert = expert_of(number)
        mask = jnp.where(column(cols, expert) == slot_lane, 1.0, 0.0).astype(BF16)
        dh_ref[0] += nn(mask, d_ref[number, 0, 0:capacity, :])
        parts = nt(mask, d_ref[number, 0, capacity:, 0:capacity])
        return jnp.where(lane == expert, jnp.sum(parts, axis=1, keepdims=True), shares)

    shares = lax.fori_loop(0, 4, take, jnp.zeros((length, LANES), F32))
    grad_n2 = dh_ref[0]

    mixes = nt(n2_high, small) + nt(n2_low, small)
    inner = nt(grad_low, small)
    with_n2 = jnp.sum(grad * n2, axis=1, keepdims=True)
    weight_copy = column(cols, kinds + ffn + 1)
    shares = jnp.where(lane == ffn + 1, weight_copy * with_n2, shares)
    share = weight_copy
    coefs = jnp.zeros((length, LANES), F32)
    for constant in range(2):
        weight = column(cols, kinds + ffn + 2 + constant)
        alpha_a, alpha_b = constant_mix(mixes, kinds + 2 * constant)
        with_vec = inner[:, kinds + 4 + constant : kinds + 5 + constant]
        share = share + weight * alpha_a
        da = weight * with_n2
        db = weight * with_vec
        mean = alpha_a * da + alpha_b * db
        shares = jnp.where(lane == ffn + 2 + constant, mean, shares)
        coefs = jnp.where(lane == kinds + 2 * constant, alpha_a * (da - mean), coefs)
        coefs = jnp.where(lane == kinds + 2 * constant + 1, alpha_b * (db - mean), coefs)
        coefs = jnp.where(lane == kinds + 4 + constant, weight * alpha_b, coefs)

    share_one = jnp.sum(shares * hot_one, axis=1, keepdims=True)
    share_two = jnp.sum(shares * hot_two, axis=1, keepdims=True)
    both = share_one + share_two
    dlogits = (share_one - gate_one * both) * hot_one + (share_two - gate_two * both) * hot_two
    coefs = jnp.where(lane < kinds, dlogits, coefs)
    back = jnp.where(lane < kinds + 4, coefs, 0.0)[:, 0:16]
    back_high, back_low = split2(back)
    grad_n2 = grad_n2 + nn(back_high, small) + nn(back_low, small) + share * grad

    coefs_t = jnp.transpose(coefs)[0:16, :]
    high, low = split2(coefs_t)
    by_n2 = nn(high, n2_high) + nn(low, n2_high)
    by_low = nn(high, n2_low)
    by_grad = nn(high, grad_low) + nn(low, grad_low)
    row = iota((16, 1), 0)
    parts = jnp.where(row < kinds, by_n2, jnp.where(row < kinds + 4, by_n2 + by_low, by_grad))
    gain_part = jnp.sum(grad_n2 * hidden * inverse, axis=0, keepdims=True)
    parts = jnp.where(row == kinds + 7, gain_part, jnp.where(row == kinds + 6, 0.0, parts))
    dlog_t = coefs_t[0:kinds, :]
    map_lane = iota((kinds, LANES), 1)
    map_part = jnp.zeros((kinds, LANES), F32)
    for j in range(kinds):
        map_part = jnp.where(
            map_lane == j, jnp.sum(dlog_t * prev_ref[j : j + 1, :], axis=1, keepdims=True), map_part
        )

    scaled = gain * grad_n2
    inner_mean = jnp.mean(scaled * hidden, axis=-1, keepdims=True)
    dh = grad + inverse * scaled - hidden * (inverse * inverse * inverse) * inner_mean
    dh_ref[0] = dh
    db = dh.astype(BF16)
    dob_ref[0] = nt(db, wo_ref[...]).astype(BF16)
    wo_part = nn(jnp.transpose(o_ref[0]), db)

    @pl.when(step == 0)
    def _():
        acc_ref[...] = wo_part
        sgrad_ref[...] = parts
        grad_map_ref[...] = map_part

    @pl.when(step > 0)
    def _():
        acc_ref[...] += wo_part
        sgrad_ref[...] += parts
        grad_map_ref[...] += map_part


def combine_kernel(
    own_ref,
    d_ref,
    pos_ref,
    aux_ref,
    prev_ref,
    h_ref,
    g_ref,
    o_ref,
    small_ref,
    wo_ref,
    dh_ref,
    dob_ref,
    grad_wo_ref,
    sgrad_ref,
    grad_map_ref,
    acc_ref,
    cols_ref,
):
    own = own_ref[0]
    step = pl.program_id(0)
    sequence_combine(
        step,
        d_ref,
        pos_ref,
        aux_ref,
        prev_ref,
        h_ref,
        g_ref,
        o_ref,
        small_ref,
        wo_ref,
        dh_ref,
        dob_ref,
        sgrad_ref,
        grad_map_ref,
        acc_ref,
        cols_ref,
        lambda number: own ^ number,
    )

    @pl.when(step == pl.num_programs(0) - 1)
    def _():
        grad_wo_ref[...] = acc_ref[...].astype(BF16)


def sequence_backward(
    step,
    x_ref,
    segments,
    q_ref,
    k_ref,
    v_ref,
    dob_ref,
    lse_ref,
    dh_ref,
    small_ref,
    w_ref,
    cos_ref,
    sin_ref,
    gin_ref,
    gain_ref,
    bias_ref,
    lse_t_ref,
    dqkv_ref,
    acc_ref,
):
    length, width = x_ref.shape[1:]
    kinds = small_ref.shape[0] - 8
    pairs = width // LANES
    lane = iota((1, LANES), 1)
    low_half = (lane % HEAD_DIM) < (HEAD_DIM // 2)
    first_head = lane < HEAD_DIM
    mask_a = jnp.where(first_head, 1.0, 0.0).astype(BF16)
    mask_b = jnp.where(first_head, 0.0, 1.0).astype(BF16)
    allowed = same_document(segments) & (
        iota((length, length), 0) // BLOCK <= iota((length, length), 1) // BLOCK
    )
    bias_ref[...] = jnp.where(allowed, 0.0, NEG)
    lse_t_ref[...] = jnp.transpose(lse_ref[0])

    def pair(h, carry):
        cols = pl.ds(pl.multiple_of(h * LANES, LANES), LANES)
        keys_t = jnp.transpose(k_ref[0, :, cols])
        grad_keys = None
        grad_values = None
        grad_queries = []
        for begin in range(0, length, BLOCK):
            end = begin + BLOCK
            queries = q_ref[0, begin:end, cols]
            outs = dob_ref[0, begin:end, cols]
            keys = k_ref[0, 0:end, cols]
            values = v_ref[0, 0:end, cols]
            queries = jnp.concatenate([queries * mask_a, queries * mask_b], axis=0)
            outs = jnp.concatenate([outs * mask_a, outs * mask_b], axis=0)
            bias = bias_ref[0:end, begin:end]
            bias = jnp.concatenate([bias, bias], axis=1)
            line = jnp.concatenate(
                [lse_t_ref[pl.ds(2 * h, 1), begin:end], lse_t_ref[pl.ds(2 * h + 1, 1), begin:end]], axis=1
            )
            chances = jnp.exp(nt(keys, queries) + bias - line)
            grad_chances = nt(values, outs)
            delta = jnp.sum(chances * grad_chances, axis=0, keepdims=True)
            grad_scores = (chances * (grad_chances - delta)).astype(BF16)
            dv = nn(chances.astype(BF16), outs)
            dk = nn(grad_scores, queries)
            dq = jnp.transpose(nn(keys_t[:, 0:end], grad_scores))
            grad_queries.append(jnp.where(first_head, dq[0:BLOCK], dq[BLOCK:]))
            if grad_keys is None:
                grad_keys, grad_values = dk, dv
            else:
                grad_keys = jnp.concatenate([grad_keys + dk[0:begin], dk[begin:]], axis=0)
                grad_values = jnp.concatenate([grad_values + dv[0:begin], dv[begin:]], axis=0)
        dq = jnp.concatenate(grad_queries, axis=0) * 0.125
        dq = dq * cos_ref[...] - swap_halves(dq, low_half) * sin_ref[...]
        dk = grad_keys * cos_ref[...] - swap_halves(grad_keys, low_half) * sin_ref[...]
        dqkv_ref[:, cols] = dq.astype(BF16)
        dqkv_ref[:, pl.ds(pl.multiple_of(width + h * LANES, LANES), LANES)] = dk.astype(BF16)
        dqkv_ref[:, pl.ds(pl.multiple_of(2 * width + h * LANES, LANES), LANES)] = grad_values.astype(BF16)
        return carry

    lax.fori_loop(0, pairs, pair, 0)

    tokens = x_ref[0].astype(F32)
    inverse = rms_scale(tokens)
    gain = small_ref[kinds + 6 : kinds + 7, :]
    a1_t = jnp.transpose((tokens * inverse * gain).astype(BF16))

    @pl.when(step == 0)
    def _():
        acc_ref[...] = jnp.zeros_like(acc_ref)

    gin_ref[0] = jnp.zeros((length, width), F32)

    def project(part, carry):
        span = pl.ds(pl.multiple_of(part * width, LANES), width)
        gin_ref[0] += nt(dqkv_ref[:, span], w_ref[:, span])
        acc_ref[:, span] += nn(a1_t, dqkv_ref[:, span])
        return carry

    lax.fori_loop(0, 3, project, 0)
    dn1 = gin_ref[0]
    scaled = gain * dn1
    inner_mean = jnp.mean(scaled * tokens, axis=-1, keepdims=True)
    gin_ref[0] = dh_ref[0] + inverse * scaled - tokens * (inverse * inverse * inverse) * inner_mean
    gain_part = jnp.broadcast_to(jnp.sum(dn1 * tokens * inverse, axis=0, keepdims=True), gain_ref.shape)

    @pl.when(step == 0)
    def _():
        gain_ref[...] = gain_part

    @pl.when(step > 0)
    def _():
        gain_ref[...] += gain_part


def small_table(depth, sgrad_ref, grad_map_ref, gain_ref):
    kinds = grad_map_ref.shape[0]
    width = sgrad_ref.shape[1]
    row = iota((16, 1), 0)
    table = jnp.where(row == kinds + 6, gain_ref[0:1, :], sgrad_ref[...])
    chosen = jnp.where(iota((LANES, width), 1) % depth == iota((LANES, width), 0), 1.0, 0.0).astype(BF16)
    maps = nn(grad_map_ref[...].astype(BF16), chosen)
    table = jnp.concatenate([table, maps, jnp.zeros((LANES - 16 - kinds, width), F32)], axis=0)
    return jnp.transpose(table).astype(BF16)


def backward_kernel(
    x_ref,
    seg_ref,
    q_ref,
    k_ref,
    v_ref,
    dob_ref,
    lse_ref,
    dh_ref,
    small_ref,
    w_ref,
    cos_ref,
    sin_ref,
    gin_ref,
    grad_w_ref,
    gain_ref,
    bias_ref,
    lse_t_ref,
    dqkv_ref,
    acc_ref,
):
    step = pl.program_id(0)
    sequence_backward(
        step,
        x_ref,
        seg_ref[0],
        q_ref,
        k_ref,
        v_ref,
        dob_ref,
        lse_ref,
        dh_ref,
        small_ref,
        w_ref,
        cos_ref,
        sin_ref,
        gin_ref,
        gain_ref,
        bias_ref,
        lse_t_ref,
        dqkv_ref,
        acc_ref,
    )

    @pl.when(step == pl.num_programs(0) - 1)
    def _():
        grad_w_ref[...] = acc_ref[...].astype(BF16)


class ReducedChunk:
    def __init__(self, here, depth, begin, value_of, send_buffer, core_buffer, buffers, out_ref, sems):
        self.here, self.depth, self.begin, self.value_of = here, depth, begin, value_of
        self.send_buffer, self.acc, self.out_ref = send_buffer, core_buffer, out_ref
        y_first, x_first, x_second, y_second, self.z_buffer, self.done, self.other = buffers
        send, recv, z_send, z_recv = sems
        planes, x, y = here.planes, here.x, here.y
        near = planes // 2
        self.half = send_buffer.shape[3] // 2
        self.mine = pl.ds(pl.multiple_of(y * self.half, LANES), self.half)
        theirs = pl.ds(pl.multiple_of((1 - y) * self.half, LANES), self.half)
        self.received = (y_first, x_first, x_second, y_second)
        acc = core_buffer
        self.swap = remote(send_buffer, acc, send.at[0], recv.at[0], here.core_peer)
        self.y_first = remote(acc.at[0:near, :, :, theirs], y_first, send.at[1], recv.at[1], here.y_peer)
        self.x_first = remote(acc.at[near:planes, 1 - x], x_first, send.at[2], recv.at[2], here.x_peer)
        self.x_second = remote(acc.at[0:near, 1 - x, :, self.mine], x_second, send.at[3], recv.at[3], here.x_peer)
        self.y_second = remote(acc.at[near:planes, x, :, theirs], y_second, send.at[4], recv.at[4], here.y_peer)
        self.along = [
            remote(
                acc.at[(here.z + k) % planes, x, :, self.mine],
                self.z_buffer.at[k - 1],
                z_send.at[k - 1],
                z_recv.at[k - 1],
                here.z_peer(k),
            )
            for k in range(1, planes)
        ]
        self.back = remote(self.done, self.other, send.at[5], recv.at[5], here.y_peer)
        self.phases = (self.first, self.second, self.third, self.fourth, self.fifth)

    def rows_of(self, z, column, core):
        return pl.ds(pl.multiple_of(self.here.block(z, column, core) * self.depth, 16), self.depth)

    def lower(self):
        def body(z, carry):
            for column in range(2):
                rows = self.rows_of(z, column, 1 - self.here.core)
                self.send_buffer[z, column] = self.value_of(rows).astype(BF16)
            return carry

        lax.fori_loop(0, self.here.planes, body, 0)

    def add(self, target, source):
        target[...] = (target[...].astype(F32) + source[...].astype(F32)).astype(BF16)

    def first(self):
        self.swap.wait_recv()

        def body(z, carry):
            for column in range(2):
                own = self.value_of(self.rows_of(z, column, self.here.core)).astype(F32)
                self.acc[z, column] = (own + self.acc[z, column].astype(F32)).astype(BF16)
            return carry

        lax.fori_loop(0, self.here.planes, body, 0)
        self.y_first.start()
        self.x_first.start()

    def second(self):
        planes = self.here.planes
        self.y_first.wait_recv()
        for z in range(planes // 2):
            for column in range(2):
                self.add(self.acc.at[z, column, :, self.mine], self.received[0].at[z, column])
        self.x_second.start()
        self.x_first.wait_recv()
        for z in range(planes // 2, planes):
            self.add(self.acc.at[z, self.here.x], self.received[1].at[z - planes // 2])
        self.y_second.start()

    def third(self):
        planes = self.here.planes
        self.x_second.wait_recv()
        for z in range(planes // 2):
            self.add(self.acc.at[z, self.here.x, :, self.mine], self.received[2].at[z])
        self.y_second.wait_recv()
        for z in range(planes // 2, planes):
            self.add(self.acc.at[z, self.here.x, :, self.mine], self.received[3].at[z - planes // 2])
        for copy in self.along:
            copy.start()

    def fourth(self):
        total = self.acc[self.here.z, self.here.x, :, self.mine].astype(F32)
        for k, copy in enumerate(self.along):
            copy.wait_recv()
            total = total + self.z_buffer[k].astype(F32)
        self.done[...] = total.astype(BF16)
        self.back.start()

    def fifth(self):
        self.back.wait_recv()
        y = self.here.y
        spot = pl.ds(pl.multiple_of(self.begin + y * self.half, LANES), self.half)
        other = pl.ds(pl.multiple_of(self.begin + (1 - y) * self.half, LANES), self.half)
        self.out_ref[:, spot] = self.done[...].astype(F32)
        self.out_ref[:, other] = self.other[...].astype(F32)
        for copy in [self.swap, self.y_first, self.x_first, self.x_second, self.y_second, self.back] + self.along:
            copy.wait_send()


def attention_columns(acc_ref, acc_wo_ref, table_ref, begin, columns, rows):
    pieces = []
    width = acc_wo_ref.shape[1]
    for start, size, ref in (
        (0, 3 * width, acc_ref),
        (3 * width, width, acc_wo_ref),
        (4 * width, LANES, table_ref),
        (4 * width + LANES, LANES, None),
    ):
        low, high = max(begin, start) - start, min(begin + columns, start + size) - start
        if low < high:
            if ref is None:
                pieces.append(jnp.zeros((rows.size, high - low), F32))
            else:
                pieces.append(ref[rows, low:high].astype(F32))
    return pieces[0] if len(pieces) == 1 else jnp.concatenate(pieces, axis=1)


def reduce_attention(chunks, free_sem):
    chunks[0].lower()
    pl.semaphore_wait(free_sem, 1)
    chunks[0].swap.start()
    for chunk in chunks[1:]:
        chunk.lower()
        chunk.swap.start()
    phases = len(chunks[0].phases)
    for step in range(len(chunks) + phases - 1):
        for number, chunk in enumerate(chunks):
            if 0 <= step - number < phases:
                chunk.phases[step - number]()


def fused_backward_kernel(
    group,
    depth,
    pos_ref,
    aux_ref,
    prev_ref,
    h_ref,
    g_ref,
    o_ref,
    x_ref,
    seg_ref,
    q_ref,
    k_ref,
    v_ref,
    lse_ref,
    small_ref,
    w_ref,
    wo_ref,
    cos_ref,
    sin_ref,
    d_ref,
    val_ref,
    gate_ref,
    up_ref,
    down_ref,
    gin_ref,
    sums_ref,
    d_in_ref,
    val_in_ref,
    gate_out_ref,
    up_out_ref,
    down_out_ref,
    acc_ref,
    acc_wo_ref,
    table_ref,
    send_buffers,
    chunk_buffers,
    cols_ref,
    dh_ref,
    dob_ref,
    sgrad_ref,
    grad_map_ref,
    gain_ref,
    bias_ref,
    lse_t_ref,
    dqkv_ref,
    rows_ref,
    gate_own,
    up_own,
    down_own,
    gate_swap,
    up_swap,
    down_swap,
    gate_near,
    up_near,
    down_near,
    gate_far,
    up_far,
    down_far,
    row_local,
    row_send,
    row_recv,
    ffn_local,
    ffn_send,
    ffn_recv,
    free_sem,
    reduce_send,
    reduce_recv,
    reduce_z_send,
    reduce_z_recv,
):
    step = pl.program_id(0)
    last = pl.num_programs(0) - 1
    here = Place(group)
    planes = here.planes
    batches = d_ref.shape[1]
    width = x_ref.shape[2]
    grads = (gate_ref, up_ref, down_ref)
    owns = (gate_own, up_own, down_own)
    swaps = (gate_swap, up_swap, down_swap)
    nears = (gate_near, up_near, down_near)
    fars = (gate_far, up_far, down_far)
    outs = (gate_out_ref, up_out_ref, down_out_ref)
    side = (here.z_peer(1), here.z_peer(planes - 1))

    def z_at(k):
        return (here.z + k) % planes

    def row_copy(kind, member, number):
        source, target = ((d_ref, d_in_ref), (val_ref, val_in_ref))[kind]
        src, dst = source.at[number, member], target.at[number, member]
        if number == 0:
            return pltpu.make_async_copy(src, dst, row_local.at[batches * 4 + member])
        return remote(
            src, dst, row_send.at[kind, member, number], row_recv.at[kind, member, number], here.plane_peers[number]
        )

    def load_rows(member, number):
        source = d_ref if number == 0 else d_in_ref
        return pltpu.make_async_copy(
            source.at[number, member], rows_ref.at[number, 0], row_local.at[member * 4 + number]
        )

    def own_copy(j):
        return pltpu.make_async_copy(grads[j].at[:, :, here.core], owns[j], ffn_local.at[j, 0])

    def swap_copy(j):
        return remote(
            grads[j].at[:, :, 1 - here.core], swaps[j], ffn_send.at[j, 0], ffn_recv.at[j, 0], here.core_peer
        )

    def near_copy(j, k):
        return remote(
            owns[j].at[z_at(2), k], nears[j].at[k], ffn_send.at[j, 1 + k], ffn_recv.at[j, 1 + k], side[k]
        )

    def far_copy(j, k):
        return remote(
            owns[j].at[z_at(1 if k == 0 else planes - 1)],
            fars[j].at[k],
            ffn_send.at[j, 3 + k],
            ffn_recv.at[j, 3 + k],
            side[k],
        )

    def plane_copy(j, number):
        x = here.x if number % 2 == 0 else 1 - here.x
        src, dst = owns[j].at[here.z, x], outs[j].at[here.expert(0)]
        if number == 0:
            return pltpu.make_async_copy(src, dst, ffn_local.at[j, 1])
        return remote(
            src, dst, ffn_send.at[j, 4 + number], ffn_recv.at[j, 4 + number], here.plane_peers[number]
        )

    def plane_arrival(j, number):
        dst = outs[j].at[here.expert(number)]
        return remote(
            dst, dst, ffn_send.at[j, 4 + number], ffn_recv.at[j, 4 + number], here.plane_peers[number]
        )

    def add(target, *sources):
        value = target[...].astype(F32)
        for source in sources:
            value = value + source[...].astype(F32)
        target[...] = value.astype(BF16)

    @pl.when(step == 0)
    def _():
        for j in range(3):
            own_copy(j).start()
        here.barrier(
            [here.core_peer, here.x_peer, here.y_peer, here.xy_peer] + [here.z_peer(k) for k in range(1, planes)]
        )
        for number in range(1, 4):
            row_copy(0, 0, number).start()
        for j in range(3):
            swap_copy(j).start()
        for j in range(3):
            own_copy(j).wait()
            swap_copy(j).wait_recv()
            for x in range(2):

                def add_core(z, carry):
                    add(owns[j].at[z, x], swaps[j].at[z, x])
                    return carry

                lax.fori_loop(0, planes, add_core, 0)
            near_copy(j, 0).start()
            near_copy(j, 1).start()
        pl.semaphore_signal(free_sem, inc=1, device_id=here.core_peer, device_id_type=MESH)

    for member in range(batches):

        @pl.when(step == member)
        def _():
            for number in range(1, 4):
                row_copy(0, member, number).wait_recv()
            if member + 1 < batches:
                for number in range(1, 4):
                    row_copy(0, member + 1, number).start()
            for number in range(4):
                row_copy(1, member, number).start()
            for number in range(4):
                load_rows(member, number).start()
            for number in range(4):
                load_rows(member, number).wait()

    sequence_combine(
        step,
        rows_ref,
        pos_ref,
        aux_ref,
        prev_ref,
        h_ref,
        g_ref,
        o_ref,
        small_ref,
        wo_ref,
        dh_ref,
        dob_ref,
        sgrad_ref,
        grad_map_ref,
        acc_wo_ref,
        cols_ref,
        here.expert,
    )

    @pl.when(step == 0)
    def _():
        for j in range(3):
            for k in range(2):
                near_copy(j, k).wait_recv()
                add(owns[j].at[z_at(1 if k == 0 else planes - 1), k], nears[j].at[k])
                far_copy(j, k).start()

    sequence_backward(
        step,
        x_ref,
        seg_ref[pl.ds(step, 1), :],
        q_ref,
        k_ref,
        v_ref,
        dob_ref,
        lse_ref,
        dh_ref,
        small_ref,
        w_ref,
        cos_ref,
        sin_ref,
        gin_ref,
        gain_ref,
        bias_ref,
        lse_t_ref,
        dqkv_ref,
        acc_ref,
    )

    @pl.when(step == last)
    def _():
        table_ref[...] = small_table(depth, sgrad_ref, grad_map_ref, gain_ref)
        for j in range(3):
            for k in range(2):
                far_copy(j, k).wait_recv()
            for x in range(2):
                add(owns[j].at[here.z, x], fars[j].at[0, x], fars[j].at[1, x])
            for number in range(4):
                plane_copy(j, number).start()
        chunks = []
        begin = 0
        for number, (send_buffer, buffers) in enumerate(zip(send_buffers, chunk_buffers)):
            columns = send_buffer.shape[3]
            home, place = (gate_swap, begin) if begin < gate_swap.shape[3] else (up_swap, begin - gate_swap.shape[3])
            chunks.append(
                ReducedChunk(
                    here,
                    depth,
                    begin,
                    functools.partial(attention_columns, acc_ref, acc_wo_ref, table_ref, begin, columns),
                    send_buffer,
                    home.at[:, :, :, place : place + columns],
                    buffers,
                    sums_ref,
                    (
                        reduce_send.at[number],
                        reduce_recv.at[number],
                        reduce_z_send.at[number],
                        reduce_z_recv.at[number],
                    ),
                )
            )
            begin += columns
        reduce_attention(chunks, free_sem)
        for j in range(3):
            swap_copy(j).wait_send()
            for k in range(2):
                near_copy(j, k).wait_send()
                far_copy(j, k).wait_send()
            plane_copy(j, 0).wait()
            for number in range(1, 4):
                plane_copy(j, number).wait_send()
                plane_arrival(j, number).wait_recv()
        for member in range(batches):
            row_copy(1, member, 0).wait()
            for number in range(1, 4):
                row_copy(0, member, number).wait_send()
                row_copy(1, member, number).wait()


def params(limit_mib):
    return pltpu.CompilerParams(vmem_limit_bytes=limit_mib * 1024 * 1024, dimension_semantics=("arbitrary",))


def rotary(length):
    halfway = HEAD_DIM // 2
    frequency = 10000.0 ** (-jnp.arange(halfway).astype(F32) / halfway)
    angles = jnp.arange(length).astype(F32)[:, None] * frequency[None, :]
    cosine, sine = jnp.cos(angles), jnp.sin(angles)
    return (
        jnp.concatenate([cosine] * 4, axis=1),
        jnp.concatenate([-sine, sine, -sine, sine], axis=1),
    )


def rotary_parts(length):
    halfway = HEAD_DIM // 2
    frequency = 10000.0 ** (-np.arange(halfway) / halfway)
    step = 32
    sign = np.tile(np.repeat([-1.0, 1.0], halfway), LANES // HEAD_DIM)

    def table(positions):
        angles = np.tile(positions[:, None] * frequency[None, :], (1, LANES // halfway))
        return np.cos(angles), np.sin(angles)

    coarse = table(np.arange(0, length, step))
    fine = table(np.arange(step))
    signs = np.broadcast_to(sign, fine[0].shape)
    return jnp.asarray(np.stack(coarse), F32), jnp.asarray(np.stack(fine + (signs,)), F32)


def local(
    reps,
    group,
    block_input,
    prev_logits,
    routes,
    segments,
    grad_out,
    gain_attn,
    w_query,
    w_key,
    w_value,
    w_output,
    gain_mix,
    router,
    route_map,
    const_proj,
    const_vec,
    w_gate,
    w_up,
    w_down,
):
    batches, length = segments.shape
    width = block_input.shape[1]
    kinds = router.shape[1]
    ffn = w_gate.shape[1]
    hidden = w_gate.shape[2]
    rows_d = w_gate.shape[0]
    rows_f = w_down.shape[0]
    capacity = length // 2
    planes = group // 4
    assert reps == 2 and ffn == 4 and group % 4 == 0
    g = lax.axis_index("grp")
    y = lax.axis_index("rep")
    core = g % 2
    x = (g // 2) % 2
    z = g // 4
    own = (2 * y + x).astype(jnp.int32)
    own_arr = own.reshape(1)

    x_flip = [(i, i ^ 2) for i in range(group)]
    core_flip = [(i, i ^ 1) for i in range(group)]
    y_flip = [(0, 1), (1, 0)]
    xy_flip = [(r * group + i, (1 - r) * group + (i ^ 2)) for r in range(2) for i in range(group)]

    def z_shift(k):
        return [(i, (i + 4 * k) % group) for i in range(group)]

    def to_plane(parts):
        return [
            parts[0],
            lax.ppermute(parts[1], "grp", x_flip),
            lax.ppermute(parts[2], "rep", y_flip),
            lax.ppermute(parts[3], ("rep", "grp"), xy_flip),
        ]

    tokens = block_input.reshape(batches, length, width)
    grads = grad_out.reshape(batches, length, width)
    route_rows = routes.T
    prev_rows = prev_logits.T
    row_spec = pl.BlockSpec((2, length), lambda b, *_: (0, b))
    prev_spec = pl.BlockSpec((kinds, length), lambda b, *_: (0, b))

    def spec_w(j):
        return pl.BlockSpec((width, width), lambda b, *_: (0, j), pipeline_mode=pl.Buffered(1))

    row_shape = jax.ShapeDtypeStruct((batches, capacity, width), BF16)
    seq_bf16 = jax.ShapeDtypeStruct((batches, length, width), BF16)
    seq_f32 = jax.ShapeDtypeStruct((batches, length, width), F32)
    fused = planes == 4 and rows_d % 16 == 0 and rows_f % 16 == 0
    if fused:
        any_space = pl.BlockSpec(memory_space=pl.ANY)
        coarse, fine = rotary_parts(length)
        smalls = [router.T, const_proj.T, const_vec.T, gain_attn[None], gain_mix[None]]
        out_struct = jax.ShapeDtypeStruct
        (
            q, k, v, o, h1, lse, aux, pos, small, cos, sin, attn, attn_o, a_rows, grad_rows, gate_full, up_full, down_full,
        ) = pl.pallas_call(
            functools.partial(fused_forward_kernel, group),
            grid=(batches,),
            in_specs=[
                per_seq((length, width)),
                whole((batches, length)),
                whole((2, batches * length)),
                prev_spec,
                whole((kinds, kinds)),
                whole((batches, length, width)),
                whole(coarse.shape),
                whole(fine.shape),
                [whole((rows_d, width))] * 4,
                [whole(part.shape) for part in smalls],
            ]
            + [any_space] * 3,
            out_specs=[per_seq((length, width))] * 5
            + [
                per_seq((length, LANES)),
                per_seq((16, length)),
                whole((batches, kinds, length)),
                whole((kinds + 8, width)),
                whole((length, LANES)),
                whole((length, LANES)),
            ]
            + [any_space] * 7,
            scratch_shapes=[
                pltpu.VMEM((width, 3 * width + 2 * LANES), BF16),
                pltpu.VMEM((width, width), BF16),
                pltpu.VMEM((length, length), F32),
                pltpu.VMEM((length, width), F32),
                pltpu.VMEM((batches, 4, capacity + 16, width), BF16),
                pltpu.VMEM((batches, 4, capacity, width), BF16),
                pltpu.VMEM((LANES, LANES), F32),
                pltpu.VMEM((kinds, LANES), F32),
                pltpu.SemaphoreType.DMA((2, 4 + 4 * planes)),
                pltpu.SemaphoreType.DMA((2, 4 + 4 * planes)),
                pltpu.SemaphoreType.DMA((3,)),
                pltpu.SemaphoreType.DMA((3, 5 + planes)),
                pltpu.SemaphoreType.DMA((3, 5 + planes)),
                pltpu.SemaphoreType.DMA((2,)),
                pltpu.SemaphoreType.DMA((2, batches)),
                pltpu.SemaphoreType.DMA((2, batches, 4)),
                pltpu.SemaphoreType.DMA((2, batches, 4)),
            ],
            out_shape=[seq_bf16] * 4
            + [
                seq_f32,
                out_struct((batches, length, LANES), F32),
                out_struct((batches, 16, length), F32),
                out_struct((batches, kinds, length), F32),
                out_struct((kinds + 8, width), F32),
                out_struct((length, LANES), F32),
                out_struct((length, LANES), F32),
                out_struct((width, 3 * width + 2 * LANES), BF16),
                out_struct((width, width), BF16),
                out_struct((4, batches, capacity + 16, width), BF16),
                out_struct((4, batches, capacity, width), BF16),
                out_struct((planes, 2, 2, rows_d, hidden), BF16),
                out_struct((planes, 2, 2, rows_d, hidden), BF16),
                out_struct((planes, 2, 2, rows_f, width), BF16),
            ],
            compiler_params=pltpu.CompilerParams(
                vmem_limit_bytes=58 * 1024 * 1024,
                dimension_semantics=("arbitrary",),
                collective_id=1,
                has_side_effects=True,
            ),
            cost_estimate=pl.CostEstimate(flops=40 * 10**9, bytes_accessed=60 * 10**6, transcendentals=10**7),
            name="fused_forward",
        )(
            tokens, segments, route_rows, prev_rows, route_map, grads, coarse, fine,
            [w_query, w_key, w_value, w_output], smalls,
            w_gate.astype(BF16).transpose(1, 0, 2),
            w_up.astype(BF16).transpose(1, 0, 2),
            w_down.astype(BF16).transpose(1, 0, 2),
        )
        gate_full = gate_full.reshape(width, hidden)
        up_full = up_full.reshape(width, hidden)
        down_full = down_full.reshape(hidden, width)
    else:
        cos, sin = rotary(length)
        small_shard = jnp.concatenate(
            [router, const_proj, const_vec, gain_attn[:, None], gain_mix[:, None]], axis=1
        ).astype(BF16)
        small_shard = jnp.pad(small_shard, ((0, 0), (0, 2 * LANES - small_shard.shape[1])))
        shard = jnp.concatenate([w.astype(BF16) for w in (w_query, w_key, w_value)] + [small_shard], axis=1)
        shard_o = w_output.astype(BF16)
        attn = lax.all_gather(shard, "grp", axis=0, tiled=True)
        attn_o = lax.all_gather(shard_o, "grp", axis=0, tiled=True)
        small = attn[:, 3 * width : 3 * width + kinds + 8].astype(F32).T

        def pick(array, expert):
            return lax.dynamic_index_in_dim(array, expert, axis=1, keepdims=False)

        def gather_expert(mine, other):
            crossed = lax.ppermute(other, "grp", x_flip)
            both = jnp.where(x == 0, jnp.stack([mine, crossed]), jnp.stack([crossed, mine]))
            pieces = [both] + [lax.ppermute(both, "grp", z_shift(k)) for k in range(1, planes)]
            stacked = jnp.stack(pieces)
            half = jnp.take(stacked, (z - jnp.arange(planes)) % planes, axis=0)
            swapped = lax.ppermute(half, "grp", core_flip)
            return jnp.where(core == 0, jnp.stack([half, swapped], axis=2), jnp.stack([swapped, half], axis=2))

        gate_up = gather_expert(
            jnp.stack([pick(w_gate, own), pick(w_up, own)]).astype(BF16),
            jnp.stack([pick(w_gate, own ^ 1), pick(w_up, own ^ 1)]).astype(BF16),
        )
        down = gather_expert(pick(w_down, own).astype(BF16), pick(w_down, own ^ 1).astype(BF16))
        gate_full = gate_up[:, :, :, 0].reshape(width, hidden)
        up_full = gate_up[:, :, :, 1].reshape(width, hidden)
        down_full = down.reshape(hidden, width)

        *grad_rows, pos = pl.pallas_call(
            grad_rows_kernel,
            grid_spec=pltpu.PrefetchScalarGridSpec(
                num_scalar_prefetch=1,
                grid=(batches,),
                in_specs=[row_spec, per_seq((length, width))],
                out_specs=[per_seq((capacity, width))] * 4 + [per_seq((kinds, length))],
            ),
            out_shape=[row_shape] * 4 + [jax.ShapeDtypeStruct((batches, kinds, length), F32)],
            compiler_params=params(32),
            cost_estimate=pl.CostEstimate(flops=4 * 10**9, bytes_accessed=8 * 10**6, transcendentals=0),
            name="grad_rows",
        )(own_arr, route_rows, grads)
        grad_rows = to_plane(grad_rows)

        q, k, v, o, h1, lse, aux, a_rows = pl.pallas_call(
            forward_kernel,
            grid_spec=pltpu.PrefetchScalarGridSpec(
                num_scalar_prefetch=1,
                grid=(batches,),
                in_specs=[
                    per_seq((length, width)),
                    per_seq((1, length)),
                    row_spec,
                    prev_spec,
                    whole((kinds, kinds)),
                    whole((kinds + 8, width)),
                    spec_w(0),
                    spec_w(1),
                    spec_w(2),
                    spec_w(0),
                    whole((length, LANES)),
                    whole((length, LANES)),
                    per_seq((kinds, length)),
                ],
                out_specs=[per_seq((length, width))] * 5
                + [per_seq((length, LANES)), per_seq((16, length))]
                + [pl.BlockSpec((4, 1, capacity + 16, width), lambda b, *_: (0, b, 0, 0))],
                scratch_shapes=[pltpu.VMEM((length, length), F32), pltpu.VMEM((length, width), F32)],
            ),
            out_shape=[seq_bf16] * 4
            + [
                seq_f32,
                jax.ShapeDtypeStruct((batches, length, LANES), F32),
                jax.ShapeDtypeStruct((batches, 16, length), F32),
            ]
            + [jax.ShapeDtypeStruct((4, batches, capacity + 16, width), BF16)],
            compiler_params=params(56),
            cost_estimate=pl.CostEstimate(flops=20 * 10**9, bytes_accessed=20 * 10**6, transcendentals=10**7),
            name="forward",
        )(own_arr, tokens, segments[:, None], route_rows, prev_rows, route_map.T, small, attn, attn, attn, attn_o, cos, sin, pos)
        a_rows = to_plane([a_rows[i] for i in range(4)])

        a_rows = jnp.stack(a_rows)
        grad_rows = jnp.stack(grad_rows)

    tile = hidden // 4
    total = 4 * batches * capacity
    any_spec = pl.BlockSpec(memory_space=pl.ANY)
    values, input_rows, grad_gate_full, grad_up_full, grad_down_full = pl.pallas_call(
        expert_kernel,
        grid=(hidden // tile,),
        in_specs=[any_spec] * 2
        + [
            pl.BlockSpec((width, tile), lambda f: (0, f)),
            pl.BlockSpec((width, tile), lambda f: (0, f)),
            pl.BlockSpec((tile, width), lambda f: (f, 0)),
        ],
        out_specs=[any_spec] * 2
        + [
            pl.BlockSpec((width, tile), lambda f: (0, f)),
            pl.BlockSpec((width, tile), lambda f: (0, f)),
            pl.BlockSpec((tile, width), lambda f: (f, 0)),
        ],
        scratch_shapes=[
            pltpu.VMEM((total + capacity, width), BF16),
            pltpu.VMEM((total + capacity, width), BF16),
            pltpu.VMEM((4 * batches, 16, capacity), BF16),
            pltpu.VMEM((width, total), BF16),
            pltpu.VMEM((width, total), BF16),
            pltpu.SMEM((4 * batches + 1,), jnp.int32),
            pltpu.VMEM((total, width), F32),
            pltpu.VMEM((total, width), F32),
            pltpu.VMEM((width, tile), F32),
            pltpu.VMEM((width, tile), F32),
            pltpu.VMEM((width, tile), F32),
            pltpu.VMEM((total + capacity, LANES), F32),
            pltpu.SemaphoreType.DMA((12 * batches,)),
        ],
        out_shape=[
            jax.ShapeDtypeStruct((4, batches, capacity, width), BF16),
            jax.ShapeDtypeStruct((4, batches, capacity + 16, width), BF16),
        ]
        + [
            jax.ShapeDtypeStruct((width, hidden), BF16),
            jax.ShapeDtypeStruct((width, hidden), BF16),
            jax.ShapeDtypeStruct((hidden, width), BF16),
        ],
        compiler_params=params(60),
        cost_estimate=pl.CostEstimate(flops=58 * 10**9, bytes_accessed=40 * 10**6, transcendentals=10**7),
        name="expert",
    )(a_rows, grad_rows, gate_full, up_full, down_full)
    if fused:
        columns = 4 * width + 2 * LANES
        once = lambda shape: pl.BlockSpec(
            (1,) + shape, lambda b, *_: (b, 0, 0), pipeline_mode=pl.Buffered(1)
        )
        wide = ((rows_d, hidden), (rows_d, hidden), (rows_f, width))
        near = planes // 2
        parts = (hidden // 2, hidden // 2, width, columns - hidden - width)
        gin, sums, _, values_in, grad_gate, grad_up, grad_down = pl.pallas_call(
            functools.partial(fused_backward_kernel, group, rows_d),
            grid=(batches,),
            in_specs=[
                per_seq((kinds, length)),
                per_seq((16, length)),
                prev_spec,
                once((length, width)),
                once((length, width)),
                once((length, width)),
                once((length, width)),
                whole((batches, length)),
                once((length, width)),
                once((length, width)),
                once((length, width)),
                once((length, LANES)),
                whole((kinds + 8, width), 1),
                pl.BlockSpec((width, 3 * width), lambda b, *_: (0, 0), pipeline_mode=pl.Buffered(1)),
                spec_w(0),
                whole((length, LANES), 1),
                whole((length, LANES), 1),
            ]
            + [any_spec] * 5,
            out_specs=[once((length, width)), whole((rows_d, columns), 1)] + [any_spec] * 5,
            out_shape=[
                seq_f32,
                jax.ShapeDtypeStruct((rows_d, columns), F32),
                jax.ShapeDtypeStruct((4, batches, capacity + 16, width), BF16),
                jax.ShapeDtypeStruct((4, batches, capacity, width), BF16),
            ]
            + [jax.ShapeDtypeStruct((4,) + shape, BF16) for shape in wide],
            scratch_shapes=[
                pltpu.VMEM((width, 3 * width), F32),
                pltpu.VMEM((width, width), F32),
                pltpu.VMEM((width, LANES), BF16),
            ]
            + [[pltpu.VMEM((planes, 2, rows_d, part), BF16) for part in parts]]
            + [
                [[
                    pltpu.VMEM((near, 2, rows_d, part // 2), BF16),
                    pltpu.VMEM((near, rows_d, part), BF16),
                    pltpu.VMEM((near, rows_d, part // 2), BF16),
                    pltpu.VMEM((near, rows_d, part // 2), BF16),
                    pltpu.VMEM((planes - 1, rows_d, part // 2), BF16),
                    pltpu.VMEM((rows_d, part // 2), BF16),
                    pltpu.VMEM((rows_d, part // 2), BF16),
                ] for part in parts]
            ]
            + [
                pltpu.VMEM((LANES, length), F32),
                pltpu.VMEM((1, length, width), F32),
                pltpu.VMEM((1, length, width), BF16),
                pltpu.VMEM((16, width), F32),
                pltpu.VMEM((kinds, LANES), F32),
                pltpu.VMEM((8, width), F32),
                pltpu.VMEM((length, length), F32),
                pltpu.VMEM((LANES, length), F32),
                pltpu.VMEM((length, 3 * width), BF16),
                pltpu.VMEM((4, 1, capacity + 16, width), BF16),
            ]
            + [pltpu.VMEM((planes, 2) + shape, BF16) for shape in wide]
            + [pltpu.VMEM((planes, 2) + shape, BF16) for shape in wide]
            + [pltpu.VMEM((2,) + shape, BF16) for shape in wide]
            + [pltpu.VMEM((2, 2) + shape, BF16) for shape in wide]
            + [
                pltpu.SemaphoreType.DMA((5 * batches,)),
                pltpu.SemaphoreType.DMA((2, batches, 4)),
                pltpu.SemaphoreType.DMA((2, batches, 4)),
                pltpu.SemaphoreType.DMA((3, 2)),
                pltpu.SemaphoreType.DMA((3, 8)),
                pltpu.SemaphoreType.DMA((3, 8)),
                pltpu.SemaphoreType.REGULAR,
                pltpu.SemaphoreType.DMA((len(parts), 6)),
                pltpu.SemaphoreType.DMA((len(parts), 6)),
                pltpu.SemaphoreType.DMA((len(parts), planes - 1)),
                pltpu.SemaphoreType.DMA((len(parts), planes - 1)),
            ],
            compiler_params=pltpu.CompilerParams(
                vmem_limit_bytes=63 * 1024 * 1024,
                dimension_semantics=("arbitrary",),
                collective_id=3,
                has_side_effects=True,
            ),
            cost_estimate=pl.CostEstimate(flops=60 * 10**9, bytes_accessed=60 * 10**6, transcendentals=10**7),
            name="fused_backward",
        )(
            pos, aux, prev_rows, h1, grads, o, tokens, segments, q, k, v, lse, small,
            attn, attn_o, cos, sin, input_rows, values,
            grad_gate_full.reshape(planes, 2, 2, rows_d, hidden),
            grad_up_full.reshape(planes, 2, 2, rows_d, hidden),
            grad_down_full.reshape(planes, 2, 2, rows_f, width),
        )
        grad_gate = grad_gate.transpose(1, 0, 2).astype(F32)
        grad_up = grad_up.transpose(1, 0, 2).astype(F32)
        grad_down = grad_down.transpose(1, 0, 2).astype(F32)
    else:
        values_in = jnp.stack(to_plane([values[i] for i in range(4)]))
        def scatter_expert(full):
            keep = lax.dynamic_index_in_dim(full, core, axis=2, keepdims=False)
            send = lax.dynamic_index_in_dim(full, 1 - core, axis=2, keepdims=False)
            half = (keep.astype(F32) + lax.ppermute(send, "grp", core_flip).astype(F32)).astype(BF16)
            summed = lax.dynamic_index_in_dim(half, z, axis=0, keepdims=False).astype(F32)
            for k in range(1, planes):
                part = lax.dynamic_index_in_dim(half, (z + k) % planes, axis=0, keepdims=False)
                summed = summed + lax.ppermute(part, "grp", z_shift(k)).astype(F32)
            summed = summed.astype(BF16)
            mine = lax.dynamic_index_in_dim(summed, x, axis=0, keepdims=False)
            other = lax.dynamic_index_in_dim(summed, 1 - x, axis=0, keepdims=False)
            arrived = to_plane([mine, other, mine, other])

            def order(first):
                return lambda: tuple(arrived[first ^ e] for e in range(4))

            return lax.switch(own, [order(i) for i in range(4)])

        grad_gate_up = scatter_expert(
            jnp.stack(
                [
                    grad_gate_full.reshape(planes, 2, 2, rows_d, hidden),
                    grad_up_full.reshape(planes, 2, 2, rows_d, hidden),
                ],
                axis=3,
            )
        )
        grad_down = scatter_expert(grad_down_full.reshape(planes, 2, 2, rows_f, width))
        grad_gate = jnp.stack([part[0] for part in grad_gate_up], axis=1).astype(F32)
        grad_up = jnp.stack([part[1] for part in grad_gate_up], axis=1).astype(F32)
        grad_down = jnp.stack(grad_down, axis=1).astype(F32)

        dh1, dob, grad_wo, sgrad, grad_map = pl.pallas_call(
            combine_kernel,
            grid_spec=pltpu.PrefetchScalarGridSpec(
                num_scalar_prefetch=1,
                grid=(batches,),
                in_specs=[pl.BlockSpec((4, 1, capacity + 16, width), lambda b, *_: (0, b, 0, 0))]
                + [
                    per_seq((kinds, length)),
                    per_seq((16, length)),
                    prev_spec,
                    per_seq((length, width)),
                    per_seq((length, width)),
                    per_seq((length, width)),
                    whole((kinds + 8, width)),
                    spec_w(0),
                ],
                out_specs=[per_seq((length, width))] * 2
                + [whole((width, width)), whole((16, width)), whole((kinds, LANES))],
                scratch_shapes=[pltpu.VMEM((width, width), F32), pltpu.VMEM((LANES, length), F32)],
            ),
            out_shape=[
                seq_f32,
                seq_bf16,
                jax.ShapeDtypeStruct((width, width), BF16),
                jax.ShapeDtypeStruct((16, width), F32),
                jax.ShapeDtypeStruct((kinds, LANES), F32),
            ],
            compiler_params=params(56),
            cost_estimate=pl.CostEstimate(flops=12 * 10**9, bytes_accessed=20 * 10**6, transcendentals=10**5),
            name="combine",
        )(own_arr, jnp.stack(to_plane([input_rows[i] for i in range(4)])), pos, aux, prev_rows, h1, grads, o, small, attn_o)

        gin, grad_attn, gain_one = pl.pallas_call(
            backward_kernel,
            grid=(batches,),
            in_specs=[
                per_seq((length, width)),
                per_seq((1, length)),
                per_seq((length, width)),
                per_seq((length, width)),
                per_seq((length, width)),
                per_seq((length, width)),
                per_seq((length, LANES)),
                per_seq((length, width)),
                whole((kinds + 8, width)),
                pl.BlockSpec((width, 3 * width), lambda b, *_: (0, 0), pipeline_mode=pl.Buffered(1)),
                whole((length, LANES)),
                whole((length, LANES)),
            ],
            out_specs=[per_seq((length, width)), whole((width, 3 * width)), whole((8, width))],
            scratch_shapes=[
                pltpu.VMEM((length, length), F32),
                pltpu.VMEM((LANES, length), F32),
                pltpu.VMEM((length, 3 * width), BF16),
                pltpu.VMEM((width, 3 * width), F32),
            ],
            out_shape=[
                seq_f32,
                jax.ShapeDtypeStruct((width, 3 * width), BF16),
                jax.ShapeDtypeStruct((8, width), F32),
            ],
            compiler_params=params(56),
            cost_estimate=pl.CostEstimate(flops=30 * 10**9, bytes_accessed=20 * 10**6, transcendentals=10**7),
            name="backward",
        )(tokens, segments[:, None], q, k, v, dob, lse, dh1, small, attn, cos, sin)

    finish_specs = dict(
        num_scalar_prefetch=1,
        grid=(batches,),
    )
    finish_in = [
        pl.BlockSpec((4, 1, capacity, width), lambda b, *_: (0, b, 0, 0)),
        per_seq((kinds, length)),
        per_seq((16, length)),
        per_seq((length, width)),
        whole((kinds + 8, width)),
    ]
    finish_cost = pl.CostEstimate(flops=4 * 10**9, bytes_accessed=12 * 10**6, transcendentals=0)
    if fused:
        small_shapes = [(rows_d, width)] * 4 + [
            (kinds, rows_d), (4, rows_d), (2, rows_d), (1, rows_d), (1, rows_d), (kinds, kinds)
        ]
        result, gq, gk, gv, go, *small_sums = pl.pallas_call(
            finish_kernel,
            grid_spec=pltpu.PrefetchScalarGridSpec(
                in_specs=finish_in + [whole((rows_d, columns))],
                out_specs=[per_seq((length, width))] + [whole(shape) for shape in small_shapes],
                scratch_shapes=[pltpu.VMEM((LANES, length), F32), pltpu.VMEM((LANES, LANES), F32)],
                **finish_specs,
            ),
            out_shape=[seq_f32] + [jax.ShapeDtypeStruct(shape, F32) for shape in small_shapes],
            compiler_params=params(60),
            cost_estimate=finish_cost,
            name="finish",
        )(own_arr, values_in, pos, aux, h1, small, sums)
        grad_router, grad_proj, grad_vec, grad_one, grad_two, map_total = small_sums
        return (
            result.reshape(batches * length, width),
            gin.reshape(batches * length, width),
            grad_one[0],
            gq,
            gk,
            gv,
            go,
            grad_two[0],
            grad_router.T,
            map_total,
            grad_proj.T,
            grad_vec.T,
            grad_gate,
            grad_up,
            grad_down,
        )

    result = pl.pallas_call(
        result_kernel,
        grid_spec=pltpu.PrefetchScalarGridSpec(
            in_specs=finish_in,
            out_specs=per_seq((length, width)),
            scratch_shapes=[pltpu.VMEM((LANES, length), F32)],
            **finish_specs,
        ),
        out_shape=seq_f32,
        compiler_params=params(40),
        cost_estimate=finish_cost,
        name="result",
    )(own_arr, values_in, pos, aux, h1, small)

    part = lax.psum_scatter(jnp.concatenate([grad_attn, grad_wo], axis=1), "grp", scatter_dimension=0, tiled=True)
    attn_total = lax.psum(part, "rep").astype(F32)
    sgrad = jnp.where(iota((16, 1), 0) == kinds + 6, gain_one[0:1], sgrad)
    packed = jnp.concatenate([sgrad, jnp.pad(grad_map, ((0, 0), (0, width - LANES)))], axis=0)
    packed = lax.psum(packed, ("rep", "grp"))
    sums = lax.dynamic_slice_in_dim(packed[0:16], g * rows_d, rows_d, axis=1).T
    map_total = packed[16:, 0:kinds].T
    return (
        result.reshape(batches * length, width),
        gin.reshape(batches * length, width),
        sums[:, kinds + 6],
        attn_total[:, 0:width],
        attn_total[:, width : 2 * width],
        attn_total[:, 2 * width : 3 * width],
        attn_total[:, 3 * width :],
        sums[:, kinds + 7],
        sums[:, 0:kinds],
        map_total,
        sums[:, kinds : kinds + 4],
        sums[:, kinds + 4 : kinds + 6],
        grad_gate,
        grad_up,
        grad_down,
    )


def solution(mesh):
    rows = P(("rep", "grp"), None)
    in_specs = (
        (rows,) * 5
        + (P("grp"),)
        + (P("grp", None),) * 4
        + (P("grp"), P("grp", None), P(), P("grp", None), P("grp", None))
        + (P("grp", None, None),) * 3
    )
    out_specs = (
        (rows,) * 2
        + (P("grp"),)
        + (P("grp", None),) * 4
        + (P("grp"), P("grp", None), P(), P("grp", None), P("grp", None))
        + (P("grp", None, None),) * 3
    )
    body = functools.partial(local, mesh.shape["rep"], mesh.shape["grp"])
    return jax.shard_map(body, mesh=mesh, in_specs=in_specs, out_specs=out_specs, check_vma=False)
```

profile of v0, /device:TPU:0, one launch (start us, length us, event | category | flops | bytes accessed | tf_op | source)
XLA Modules:
  0.0 366.6 jit_solution(1760837714359185879)
XLA Ops:
  0.6 0.0 copy-start.1
  0.7 4.8 %fusion = (bf16[4,48,2048]{2,1,0:T(8,128)(2,1)}, bf16[4,48,2048]{2,1,0:T(8,128)(2,1)}) fusion(f32[48,4,2048]{2,1,0:T(4,128)} %param.35, f32[48,4,2048]{2,1,0:T(4,128)} %param.36), kind=kLoop, calls=%fused_computation.6 | loop fusion | bytes 4718592 | tf_op jit(solution)/shard_map/transpose | solution.py:1873
  5.5 0.0 copy-done.1
  5.5 1.1 copy.50
  6.6 116.7 %fused_forward.1 = (bf16[2,512,768]{2,1,0:T(8,128)(2,1)}, bf16[2,512,768]{2,1,0:T(8,128)(2,1)}, bf16[2,512,768]{2,1,0:T(8,128)(2,1)}, bf16[2,512,768]{2,1,0:T(8,...) custom-call(bf16[2,512,768]{2,1,0:T(8,128)(2,1)} %bitcast.38, ...), custom_call_target="tpu_custom_call" | custom-call | flops 40000000000 | bytes 60000000 | tf_op jit(solution)/shard_map/fused_forward/pallas_call | solution.py:1800
  123.3 51.3 %expert.1 = (bf16[4,2,256,768]{3,2,1,0:T(8,128)(2,1)}, bf16[4,2,272,768]{3,2,1,0:T(8,128)(2,1)}, bf16[768,2048]{1,0:T(8,128)(2,1)}, bf16[768,2048]{1,0:T(8,128)(2,1)}, bf16[2048,768]{1,0:T(8,128)(2,1)}) custom-call(bf16[4,2,272,768]{3,2,1,0:T(8,128)(2,1)} %get-tuple-element.68.a_ref, bf16[4,2,256,768]{3,2,1,0:T(8,128)(2,1)} %get-tuple-element.69.g_ref, ...), custom_call_target="tpu_custom_call" | custom-call | flops 57999998976 | bytes 40000000 | tf_op jit(solution)/shard_map/expert/pallas_call | solution.py:1972
  174.6 173.0 %fused_backward.1 = (f32[2,512,768]{2,1,0:T(8,128)}, f32[48,3328]{1,0:T(8,128)}, bf16[4,2,272,768]{3,2,1,0:T(8,128)(2,1)}, bf16[4,2,256,768]{3,2,1,0:T(8,128)(2,...) custom-call(f32[2,8,512]{2,1,0:T(8,128)} %get-tuple-element.55.pos_ref, ...), custom_call_target="tpu_custom_call" | custom-call | flops 60000002048 | bytes 60000000 | tf_op jit(solution)/shard_map/fused_backward/pallas_call | solution.py:2023
  347.6 0.0 copy-start.4
  347.6 10.3 %finish.1 = (f32[2,512,768]{2,1,0:T(8,128)}, f32[48,768]{1,0:T(8,128)}, f32[48,768]{1,0:T(8,128)}, f32[48,768]{1,0:T(8,128)}, f32[48,768]{1,0:T(8,128)}, /*index...) custom-call(s32[1]{0:T(128)} %bitcast.own_ref, ...), custom_call_target="tpu_custom_call" | custom-call | flops 4000000000 | bytes 12000000 | tf_op jit(solution)/shard_map/finish/pallas_call | solution.py:2234
  357.9 0.0 copy-done.4
  357.9 0.2 convert_bitcast_fusion.2
  358.1 0.0 copy-start.3
  358.1 2.2 copy.38
  360.2 0.0 copy-done.3
  360.2 0.2 convert_bitcast_fusion.1
  360.4 0.0 copy-start.2
  360.4 2.2 copy.39
  362.6 0.0 copy-done.2
  362.6 0.1 convert_bitcast_fusion
  362.7 0.0 copy-start
  362.7 2.2 copy.40
  364.9 0.0 copy-done
  364.9 1.7 copy.52
Async XLA Ops:
  0.6 4.8 %copy-start.1 = (f32[128,4,768]{2,1,0:T(4,128)S(1)}, f32[128,4,768]{2,1,0:T(4,128)}, u32[]{:S(2)}) copy-start(f32[128,4,768]{2,1,0:T(4,128)} %param.37) | copy-start | bytes 4718596
  347.6 10.3 %copy-start.4 = (bf16[4,48,2048]{2,1,0:T(8,128)(2,1)S(1)}, bf16[4,48,2048]{2,1,0:T(8,128)(2,1)}, u32[]{:S(2)}) copy-start(bf16[4,48,2048]{2,1,0:T(8,128)(2,1)} %get-tuple-element.92) | copy-start | bytes 2359300
  358.1 2.2 copy-start.3
  360.4 2.2 copy-start.2
  362.7 2.2 copy-start
where the time goes:
time: 364 us; the launch traced here: 367 us
  Pallas kernels  351 us (96%)
  local copies, waits for them, and re-layouts  14.1 us (4%)
    pallas_call x1, Pallas kernels, local(): pl.pallas_call(functools.partial(fused_backward_kernel, group, rows_d), g...  173 us
    pallas_call x1, Pallas kernels, local(): pl.pallas_call(functools.partial(fused_forward_kernel, group), grid=(batc...  117 us
    pallas_call x1, Pallas kernels, local(): pl.pallas_call(expert_kernel, grid=(hidden // tile,), in_specs=[any_spec]...  51.3 us
    pallas_call x1, Pallas kernels, local(): pl.pallas_call(finish_kernel, grid_spec=pltpu.PrefetchScalarGridSpec(in_s...  10.3 us
    unnamed x15, local copies, waits for them, and re-layouts  9.26 us

commit v1 on v0

--- a/solution.py
+++ b/solution.py
@@ -169,7 +169,7 @@
             o_ref[0, begin:end, cols] = jnp.where(first_head, outs[0], outs[1]).astype(BF16)
         return carry
 
-    lax.fori_loop(0, pairs, pair, 0)
+    lax.fori_loop(0, pairs, pair, 0, unroll=2)
 
     hidden = tokens + nn(o_ref[0], wo_ref[...])
     h_ref[0] = hidden
@@ -951,6 +951,7 @@
     acc_ref,
     cols_ref,
     expert_of,
+    arrived=lambda: None,
 ):
     length, width = h_ref.shape[1:]
     kinds = pos_ref.shape[1]
@@ -972,19 +973,7 @@
     hot_one = jnp.where(column(cols, 2 * kinds + 2) == ids, 1.0, 0.0)
     hot_two = jnp.where(column(cols, 2 * kinds + 3) == ids, 1.0, 0.0)
 
-    dh_ref[0] = jnp.zeros((length, width), F32)
-    slot_lane = iota((1, capacity), 1).astype(F32)
-
-    def take(number, shares):
-        expert = expert_of(number)
-        mask = jnp.where(column(cols, expert) == slot_lane, 1.0, 0.0).astype(BF16)
-        dh_ref[0] += nn(mask, d_ref[number, 0, 0:capacity, :])
-        parts = nt(mask, d_ref[number, 0, capacity:, 0:capacity])
-        return jnp.where(lane == expert, jnp.sum(parts, axis=1, keepdims=True), shares)
-
-    shares = lax.fori_loop(0, 4, take, jnp.zeros((length, LANES), F32))
-    grad_n2 = dh_ref[0]
-
+    shares = jnp.zeros((length, LANES), F32)
     mixes = nt(n2_high, small) + nt(n2_low, small)
     inner = nt(grad_low, small)
     with_n2 = jnp.sum(grad * n2, axis=1, keepdims=True)
@@ -1004,6 +993,20 @@
         coefs = jnp.where(lane == kinds + 2 * constant, alpha_a * (da - mean), coefs)
         coefs = jnp.where(lane == kinds + 2 * constant + 1, alpha_b * (db - mean), coefs)
         coefs = jnp.where(lane == kinds + 4 + constant, weight * alpha_b, coefs)
+
+    arrived()
+    dh_ref[0] = jnp.zeros((length, width), F32)
+    slot_lane = iota((1, capacity), 1).astype(F32)
+
+    def take(number, shares):
+        expert = expert_of(number)
+        mask = jnp.where(column(cols, expert) == slot_lane, 1.0, 0.0).astype(BF16)
+        dh_ref[0] += nn(mask, d_ref[number, 0, 0:capacity, :])
+        parts = nt(mask, d_ref[number, 0, capacity:, 0:capacity])
+        return jnp.where(lane == expert, jnp.sum(parts, axis=1, keepdims=True), shares)
+
+    shares = lax.fori_loop(0, 4, take, shares)
+    grad_n2 = dh_ref[0]
 
     share_one = jnp.sum(shares * hot_one, axis=1, keepdims=True)
     share_two = jnp.sum(shares * hot_two, axis=1, keepdims=True)
@@ -1098,15 +1101,22 @@
         grad_wo_ref[...] = acc_ref[...].astype(BF16)
 
 
+def backward_tables(segments, lse_ref, bias_ref, lse_t_ref):
+    length = lse_ref.shape[1]
+    allowed = same_document(segments) & (
+        iota((length, length), 0) // BLOCK <= iota((length, length), 1) // BLOCK
+    )
+    bias_ref[...] = jnp.where(allowed, 0.0, NEG)
+    lse_t_ref[...] = jnp.transpose(lse_ref[0])
+
+
 def sequence_backward(
     step,
     x_ref,
-    segments,
     q_ref,
     k_ref,
     v_ref,
     dob_ref,
-    lse_ref,
     dh_ref,
     small_ref,
     w_ref,
@@ -1118,6 +1128,7 @@
     lse_t_ref,
     dqkv_ref,
     acc_ref,
+    between=lambda: None,
 ):
     length, width = x_ref.shape[1:]
     kinds = small_ref.shape[0] - 8
@@ -1127,11 +1138,6 @@
     first_head = lane < HEAD_DIM
     mask_a = jnp.where(first_head, 1.0, 0.0).astype(BF16)
     mask_b = jnp.where(first_head, 0.0, 1.0).astype(BF16)
-    allowed = same_document(segments) & (
-        iota((length, length), 0) // BLOCK <= iota((length, length), 1) // BLOCK
-    )
-    bias_ref[...] = jnp.where(allowed, 0.0, NEG)
-    lse_t_ref[...] = jnp.transpose(lse_ref[0])
 
     def pair(h, carry):
         cols = pl.ds(pl.multiple_of(h * LANES, LANES), LANES)
@@ -1173,7 +1179,8 @@
         dqkv_ref[:, pl.ds(pl.multiple_of(2 * width + h * LANES, LANES), LANES)] = grad_values.astype(BF16)
         return carry
 
-    lax.fori_loop(0, pairs, pair, 0)
+    lax.fori_loop(0, pairs, pair, 0, unroll=2)
+    between()
 
     tokens = x_ref[0].astype(F32)
     inverse = rms_scale(tokens)
@@ -1241,15 +1248,14 @@
     acc_ref,
 ):
     step = pl.program_id(0)
+    backward_tables(seg_ref[0], lse_ref, bias_ref, lse_t_ref)
     sequence_backward(
         step,
         x_ref,
-        seg_ref[0],
         q_ref,
         k_ref,
         v_ref,
         dob_ref,
-        lse_ref,
         dh_ref,
         small_ref,
         w_ref,
@@ -1387,7 +1393,7 @@
     return pieces[0] if len(pieces) == 1 else jnp.concatenate(pieces, axis=1)
 
 
-def reduce_attention(chunks, free_sem):
+def reduce_attention(chunks, free_sem, beside):
     chunks[0].lower()
     pl.semaphore_wait(free_sem, 1)
     chunks[0].swap.start()
@@ -1399,6 +1405,8 @@
         for number, chunk in enumerate(chunks):
             if 0 <= step - number < phases:
                 chunk.phases[step - number]()
+        if step in beside:
+            beside[step]()
 
 
 def fused_backward_kernel(
@@ -1572,22 +1580,24 @@
             near_copy(j, 1).start()
         pl.semaphore_signal(free_sem, inc=1, device_id=here.core_peer, device_id_type=MESH)
 
-    for member in range(batches):
-
-        @pl.when(step == member)
-        def _():
-            for number in range(1, 4):
-                row_copy(0, member, number).wait_recv()
-            if member + 1 < batches:
+    def arrived():
+        for member in range(batches):
+
+            @pl.when(step == member)
+            def _():
                 for number in range(1, 4):
-                    row_copy(0, member + 1, number).start()
-            for number in range(4):
-                row_copy(1, member, number).start()
-            for number in range(4):
-                load_rows(member, number).start()
-            for number in range(4):
-                load_rows(member, number).wait()
-
+                    row_copy(0, member, number).wait_recv()
+                if member + 1 < batches:
+                    for number in range(1, 4):
+                        row_copy(0, member + 1, number).start()
+                for number in range(4):
+                    row_copy(1, member, number).start()
+                for number in range(4):
+                    load_rows(member, number).start()
+                for number in range(4):
+                    load_rows(member, number).wait()
+
+    backward_tables(seg_ref[pl.ds(step, 1), :], lse_ref, bias_ref, lse_t_ref)
     sequence_combine(
         step,
         rows_ref,
@@ -1606,25 +1616,42 @@
         acc_wo_ref,
         cols_ref,
         here.expert,
+        arrived,
     )
 
-    @pl.when(step == 0)
-    def _():
-        for j in range(3):
-            for k in range(2):
-                near_copy(j, k).wait_recv()
-                add(owns[j].at[z_at(1 if k == 0 else planes - 1), k], nears[j].at[k])
-                far_copy(j, k).start()
+    def start_far(j):
+        far_copy(j, 0).start()
+        far_copy(j, 1).start()
+
+    def finish_far(j):
+        for k in range(2):
+            far_copy(j, k).wait_recv()
+        for x in range(2):
+            add(owns[j].at[here.z, x], fars[j].at[0, x], fars[j].at[1, x])
+        for number in range(4):
+            plane_copy(j, number).start()
+
+    def between():
+        @pl.when(step == 0)
+        def _():
+            for j in range(3):
+                for k in range(2):
+                    near_copy(j, k).wait_recv()
+                    add(owns[j].at[z_at(1 if k == 0 else planes - 1), k], nears[j].at[k])
+            start_far(0)
+
+        @pl.when(step == last)
+        def _():
+            finish_far(0)
+            start_far(2)
 
     sequence_backward(
         step,
         x_ref,
-        seg_ref[pl.ds(step, 1), :],
         q_ref,
         k_ref,
         v_ref,
         dob_ref,
-        lse_ref,
         dh_ref,
         small_ref,
         w_ref,
@@ -1636,18 +1663,16 @@
         lse_t_ref,
         dqkv_ref,
         acc_ref,
+        between,
     )
+
+    @pl.when(step == 0)
+    def _():
+        start_far(1)
 
     @pl.when(step == last)
     def _():
         table_ref[...] = small_table(depth, sgrad_ref, grad_map_ref, gain_ref)
-        for j in range(3):
-            for k in range(2):
-                far_copy(j, k).wait_recv()
-            for x in range(2):
-                add(owns[j].at[here.z, x], fars[j].at[0, x], fars[j].at[1, x])
-            for number in range(4):
-                plane_copy(j, number).start()
         chunks = []
         begin = 0
         for number, (send_buffer, buffers) in enumerate(zip(send_buffers, chunk_buffers)):
@@ -1672,7 +1697,7 @@
                 )
             )
             begin += columns
-        reduce_attention(chunks, free_sem)
+        reduce_attention(chunks, free_sem, {0: lambda: finish_far(1), len(chunks): lambda: finish_far(2)})
         for j in range(3):
             swap_copy(j).wait_send()
             for k in range(2):

time: 364 us -> 346 us (0.951)
  Pallas kernels: 351 us -> 330 us
    pallas_call x1, Pallas kernels: 173 us -> 153 us  [local(): pl.pallas_call(functools.partial(fused_backward_kernel, group, rows_d), g...]
where the time goes in v1:
time: 346 us; the launch traced here: 345 us
  Pallas kernels  330 us (95%)
  local copies, waits for them, and re-layouts  14.1 us (4%)
    pallas_call x1, Pallas kernels, local(): pl.pallas_call(functools.partial(fused_backward_kernel, group, rows_d), g...  153 us
    pallas_call x1, Pallas kernels, local(): pl.pallas_call(functools.partial(fused_forward_kernel, group), grid=(batc...  115 us
    pallas_call x1, Pallas kernels, local(): pl.pallas_call(expert_kernel, grid=(hidden // tile,), in_specs=[any_spec]...  51.3 us
    pallas_call x1, Pallas kernels, local(): pl.pallas_call(finish_kernel, grid_spec=pltpu.PrefetchScalarGridSpec(in_s...  10.3 us
    unnamed x15, local copies, waits for them, and re-layouts  9.26 us

profile of v1, /device:TPU:0, one launch (start us, length us, event | category | flops | bytes accessed | tf_op | source)
XLA Modules:
  0.0 345.3 jit_solution(15190640170343285611)
XLA Ops:
  0.6 0.0 copy-start.1
  0.7 4.8 %fusion = (bf16[4,48,2048]{2,1,0:T(8,128)(2,1)}, bf16[4,48,2048]{2,1,0:T(8,128)(2,1)}) fusion(f32[48,4,2048]{2,1,0:T(4,128)} %param.35, f32[48,4,2048]{2,1,0:T(4,128)} %param.36), kind=kLoop, calls=%fused_computation.6 | loop fusion | bytes 4718592 | tf_op jit(solution)/shard_map/transpose | solution.py:1898
  5.5 0.0 copy-done.1
  5.5 1.1 copy.50
  6.6 115.4 %fused_forward.1 = (bf16[2,512,768]{2,1,0:T(8,128)(2,1)}, bf16[2,512,768]{2,1,0:T(8,128)(2,1)}, bf16[2,512,768]{2,1,0:T(8,128)(2,1)}, bf16[2,512,768]{2,1,0:T(8,...) custom-call(bf16[2,512,768]{2,1,0:T(8,128)(2,1)} %bitcast.38, ...), custom_call_target="tpu_custom_call" | custom-call | flops 40000000000 | bytes 60000000 | tf_op jit(solution)/shard_map/fused_forward/pallas_call | solution.py:1825
  121.9 51.3 %expert.1 = (bf16[4,2,256,768]{3,2,1,0:T(8,128)(2,1)}, bf16[4,2,272,768]{3,2,1,0:T(8,128)(2,1)}, bf16[768,2048]{1,0:T(8,128)(2,1)}, bf16[768,2048]{1,0:T(8,128)(2,1)}, bf16[2048,768]{1,0:T(8,128)(2,1)}) custom-call(bf16[4,2,272,768]{3,2,1,0:T(8,128)(2,1)} %get-tuple-element.68.a_ref, bf16[4,2,256,768]{3,2,1,0:T(8,128)(2,1)} %get-tuple-element.69.g_ref, ...), custom_call_target="tpu_custom_call" | custom-call | flops 57999998976 | bytes 40000000 | tf_op jit(solution)/shard_map/expert/pallas_call | solution.py:1997
  173.3 153.0 %fused_backward.1 = (f32[2,512,768]{2,1,0:T(8,128)}, f32[48,3328]{1,0:T(8,128)}, bf16[4,2,272,768]{3,2,1,0:T(8,128)(2,1)}, bf16[4,2,256,768]{3,2,1,0:T(8,128)(2,...) custom-call(f32[2,8,512]{2,1,0:T(8,128)} %get-tuple-element.55.pos_ref, ...), custom_call_target="tpu_custom_call" | custom-call | flops 60000002048 | bytes 60000000 | tf_op jit(solution)/shard_map/fused_backward/pallas_call | solution.py:2048
  326.3 0.0 copy-start.4
  326.3 10.3 %finish.1 = (f32[2,512,768]{2,1,0:T(8,128)}, f32[48,768]{1,0:T(8,128)}, f32[48,768]{1,0:T(8,128)}, f32[48,768]{1,0:T(8,128)}, f32[48,768]{1,0:T(8,128)}, /*index...) custom-call(s32[1]{0:T(128)} %bitcast.own_ref, ...), custom_call_target="tpu_custom_call" | custom-call | flops 4000000000 | bytes 12000000 | tf_op jit(solution)/shard_map/finish/pallas_call | solution.py:2259
  336.6 0.0 copy-done.4
  336.6 0.2 convert_bitcast_fusion.2
  336.8 0.0 copy-start.3
  336.8 2.2 copy.38
  339.0 0.0 copy-done.3
  339.0 0.2 convert_bitcast_fusion.1
  339.1 0.0 copy-start.2
  339.2 2.2 copy.39
  341.3 0.0 copy-done.2
  341.3 0.1 convert_bitcast_fusion
  341.5 0.0 copy-start
  341.5 2.2 copy.40
  343.6 0.0 copy-done
  343.6 1.7 copy.52
Async XLA Ops:
  0.6 4.8 %copy-start.1 = (f32[128,4,768]{2,1,0:T(4,128)S(1)}, f32[128,4,768]{2,1,0:T(4,128)}, u32[]{:S(2)}) copy-start(f32[128,4,768]{2,1,0:T(4,128)} %param.37) | copy-start | bytes 4718596
  326.3 10.3 %copy-start.4 = (bf16[4,48,2048]{2,1,0:T(8,128)(2,1)S(1)}, bf16[4,48,2048]{2,1,0:T(8,128)(2,1)}, u32[]{:S(2)}) copy-start(bf16[4,48,2048]{2,1,0:T(8,128)(2,1)} %get-tuple-element.92) | copy-start | bytes 2359300
  336.8 2.2 copy-start.3
  339.1 2.2 copy-start.2
  341.5 2.2 copy-start

commit v2 on v1

--- a/solution.py
+++ b/solution.py
@@ -921,7 +921,7 @@
         out_ref[0] += column(cols, kinds + expert) * nn(mask, v_ref[number, 0])
         return carry
 
-    lax.fori_loop(0, 4, take, 0)
+    lax.fori_loop(0, 4, take, 0, unroll=2)
     result = out_ref[0]
     mixes = nt(n2_high, small) + nt(n2_low, small)
     share = column(cols, kinds + ffn + 1)
@@ -1697,7 +1697,7 @@
                 )
             )
             begin += columns
-        reduce_attention(chunks, free_sem, {0: lambda: finish_far(1), len(chunks): lambda: finish_far(2)})
+        reduce_attention(chunks, free_sem, {2: lambda: finish_far(1), len(chunks) + 1: lambda: finish_far(2)})
         for j in range(3):
             swap_copy(j).wait_send()
             for k in range(2):

time: 346 us -> 344 us (level); the launches traced: 345 us -> 337 us
  Pallas kernels: 330 us -> 322 us
    pallas_call x1, Pallas kernels: 153 us -> 136 us  [local(): pl.pallas_call(functools.partial(fused_backward_kernel, group, rows_d), g...]
    pallas_call x1, Pallas kernels: 51.3 us -> 60.6 us  [local(): pl.pallas_call(expert_kernel, grid=(hidden // tile,), in_specs=[any_spec]...]
where the time goes in v2:
time: 344 us; the launch traced here: 337 us
  Pallas kernels  322 us (94%)
  local copies, waits for them, and re-layouts  14.1 us (4%)
    pallas_call x1, Pallas kernels, local(): pl.pallas_call(functools.partial(fused_backward_kernel, group, rows_d), g...  136 us
    pallas_call x1, Pallas kernels, local(): pl.pallas_call(functools.partial(fused_forward_kernel, group), grid=(batc...  115 us
    pallas_call x1, Pallas kernels, local(): pl.pallas_call(expert_kernel, grid=(hidden // tile,), in_specs=[any_spec]...  60.6 us
    pallas_call x1, Pallas kernels, local(): pl.pallas_call(finish_kernel, grid_spec=pltpu.PrefetchScalarGridSpec(in_s...  9.39 us
    unnamed x15, local copies, waits for them, and re-layouts  9.26 us

profile of v2, /device:TPU:0, one launch (start us, length us, event | category | flops | bytes accessed | tf_op | source)
XLA Modules:
  0.0 337.1 jit_solution(2780219404971711673)
XLA Ops:
  0.6 0.0 copy-start.1
  0.7 4.8 %fusion = (bf16[4,48,2048]{2,1,0:T(8,128)(2,1)}, bf16[4,48,2048]{2,1,0:T(8,128)(2,1)}) fusion(f32[48,4,2048]{2,1,0:T(4,128)} %param.35, f32[48,4,2048]{2,1,0:T(4,128)} %param.36), kind=kLoop, calls=%fused_computation.6 | loop fusion | bytes 4718592 | tf_op jit(solution)/shard_map/transpose | solution.py:1898
  5.5 0.0 copy-done.1
  5.5 1.1 copy.50
  6.6 115.4 %fused_forward.1 = (bf16[2,512,768]{2,1,0:T(8,128)(2,1)}, bf16[2,512,768]{2,1,0:T(8,128)(2,1)}, bf16[2,512,768]{2,1,0:T(8,128)(2,1)}, bf16[2,512,768]{2,1,0:T(8,...) custom-call(bf16[2,512,768]{2,1,0:T(8,128)(2,1)} %bitcast.38, ...), custom_call_target="tpu_custom_call" | custom-call | flops 40000000000 | bytes 60000000 | tf_op jit(solution)/shard_map/fused_forward/pallas_call | solution.py:1825
  121.9 60.6 %expert.1 = (bf16[4,2,256,768]{3,2,1,0:T(8,128)(2,1)}, bf16[4,2,272,768]{3,2,1,0:T(8,128)(2,1)}, bf16[768,2048]{1,0:T(8,128)(2,1)}, bf16[768,2048]{1,0:T(8,128)(2,1)}, bf16[2048,768]{1,0:T(8,128)(2,1)}) custom-call(bf16[4,2,272,768]{3,2,1,0:T(8,128)(2,1)} %get-tuple-element.68.a_ref, bf16[4,2,256,768]{3,2,1,0:T(8,128)(2,1)} %get-tuple-element.69.g_ref, ...), custom_call_target="tpu_custom_call" | custom-call | flops 57999998976 | bytes 40000000 | tf_op jit(solution)/shard_map/expert/pallas_call | solution.py:1997
  182.6 136.4 %fused_backward.1 = (f32[2,512,768]{2,1,0:T(8,128)}, f32[48,3328]{1,0:T(8,128)}, bf16[4,2,272,768]{3,2,1,0:T(8,128)(2,1)}, bf16[4,2,256,768]{3,2,1,0:T(8,128)(2,...) custom-call(f32[2,8,512]{2,1,0:T(8,128)} %get-tuple-element.55.pos_ref, ...), custom_call_target="tpu_custom_call" | custom-call | flops 60000002048 | bytes 60000000 | tf_op jit(solution)/shard_map/fused_backward/pallas_call | solution.py:2048
  319.0 0.0 copy-start.4
  319.0 9.4 %finish.1 = (f32[2,512,768]{2,1,0:T(8,128)}, f32[48,768]{1,0:T(8,128)}, f32[48,768]{1,0:T(8,128)}, f32[48,768]{1,0:T(8,128)}, f32[48,768]{1,0:T(8,128)}, /*index...) custom-call(s32[1]{0:T(128)} %bitcast.own_ref, ...), custom_call_target="tpu_custom_call" | custom-call | flops 4000000000 | bytes 12000000 | tf_op jit(solution)/shard_map/finish/pallas_call | solution.py:2259
  328.4 0.0 copy-done.4
  328.4 0.2 convert_bitcast_fusion.2
  328.6 0.0 copy-start.3
  328.6 2.2 copy.38
  330.8 0.0 copy-done.3
  330.8 0.2 convert_bitcast_fusion.1
  330.9 0.0 copy-start.2
  330.9 2.2 copy.39
  333.1 0.0 copy-done.2
  333.1 0.1 convert_bitcast_fusion
  333.2 0.0 copy-start
  333.3 2.2 copy.40
  335.4 0.0 copy-done
  335.4 1.7 copy.52
Async XLA Ops:
  0.6 4.8 %copy-start.1 = (f32[128,4,768]{2,1,0:T(4,128)S(1)}, f32[128,4,768]{2,1,0:T(4,128)}, u32[]{:S(2)}) copy-start(f32[128,4,768]{2,1,0:T(4,128)} %param.37) | copy-start | bytes 4718596
  319.0 9.4 %copy-start.4 = (bf16[4,48,2048]{2,1,0:T(8,128)(2,1)S(1)}, bf16[4,48,2048]{2,1,0:T(8,128)(2,1)}, u32[]{:S(2)}) copy-start(bf16[4,48,2048]{2,1,0:T(8,128)(2,1)} %get-tuple-element.92) | copy-start | bytes 2359300
  328.6 2.2 copy-start.3
  330.9 2.2 copy-start.2
  333.2 2.2 copy-start
